TPU v7x, 32 devices: a whole 2x2x4 slice. The times are simulated.
32 devices in a mesh: gx: 4 (over y, x), gy: 4 (over z), gz: 2 (over core).
Axes of the slice: x: 2, y: 2, z: 4, core: 2. Of those that a mesh axis runs over, the one named last changes fastest.
Arguments:
- checkpoint: float32 [5, 32, 32, 512], P(None, 'gz', 'gx', 'gy'), may hold values from -0.6 to 0.6
- gruneisen: float32 [32, 32, 512], P('gz', 'gx', 'gy'), may hold values from 1 to 3
- switch: int32 [2, 32, 32, 512], P(None, 'gz', 'gx', 'gy'), may hold values 0 or 1
- probes: int32 [8192], P(('gx', 'gy', 'gz')), may hold values from 0 to 16383
- observed: float32 [8192], P(('gx', 'gy', 'gz')), may hold values from -1 to 1
Outputs:
- direction: float32 [32, 32, 512], P('gz', 'gx', 'gy')
- misfit: float32 [], replicated
Inputs may be any that keep to these rules, and one draw needn't show every extreme that they name: `probes`: entry k names a cell of the block of the device that holds entry k, as the flat index (z * 8 + x) * 128 + y within that block; cells may repeat.
All inputs are finite; a program needn't handle non-finite values. No bound on the sum of `switch` on one device may be relied on, other than what follows from the above.
Results may differ from a plain program's by a relative error of at most 0.0001.
Values sent between devices are 32-bit elements; how exact they have to be, the bound alone decides.
A program may use at most 64 MiB of HBM per device.

v0:
```python
import functools
import math

import jax
import jax.numpy as jnp
from jax import lax
from jax.experimental import pallas as pl
from jax.experimental.pallas import tpu as pltpu
from jax.sharding import PartitionSpec as P

BULK = 2.0
SLOPE = 1.5
SIGNAL = 2.5
DT = 0.1
QUAD = 4.0
EPS = 1e-12
AXES = ("gx", "gy", "gz")
HI = lax.Precision.HIGHEST


def kernel(
    sizes, st, ga, sw, pr_in, ob_in, grad_out, mis_out, scale_out,
    se0, se1, ge, we, xs0, xg, xw, xs1, xq, q1, xv0, vh0, xe, pr, ob, en0, ve0, xl, xm, ze, az, bz, zm, kap, kah, gam2, lam,
    yp1, yl1, yu1, yp2, yl2, yu2, yp3, yl3, yu3, yp4, yl4, yu4, cnt, sob, vel, hot_a, hot_b, grad,
    mine, ar, local_sem, send_sem, recv_sem, all_send, all_recv,
):
    nz, nx, ny = ga.shape
    count = dict(zip(AXES, sizes))
    index = {a: lax.axis_index(a) for a in AXES}
    total = math.prod(sizes)
    me = (index["gx"] * sizes[1] + index["gy"]) * sizes[2] + index["gz"]
    group = 4
    per = ny // (group * nz)

    loads = [
        pltpu.make_async_copy(st, se0.at[:, pl.ds(2, nz)], local_sem.at[0]),
        pltpu.make_async_copy(ga, ge.at[pl.ds(2, nz)], local_sem.at[1]),
        pltpu.make_async_copy(sw, we.at[:, pl.ds(2, nz)], local_sem.at[2]),
        pltpu.make_async_copy(pr_in, pr, local_sem.at[3]),
        pltpu.make_async_copy(ob_in, ob, local_sem.at[4]),
    ]
    for copy in loads:
        copy.start()

    barrier = pltpu.get_barrier_semaphore()

    def spot_of(k):
        if isinstance(k, int):
            parts = (k // (sizes[1] * sizes[2]), k // sizes[2] % sizes[1], k % sizes[2])
        else:
            parts = (k // (sizes[1] * sizes[2]), lax.rem(k // sizes[2], sizes[1]), lax.rem(k, sizes[2]))
        return {a: lax.rem(index[a] + parts[i], count[a]) for i, a in enumerate(AXES)}

    def flat(where):
        return (where["gx"] * sizes[1] + where["gy"]) * sizes[2] + where["gz"]

    def each_peer(body):
        if total <= 64:
            for k in range(1, total):
                body(k)
        else:
            def step(k, carry):
                body(k)
                return carry
            lax.fori_loop(1, total, step, 0)

    each_peer(lambda k: pl.semaphore_signal(
        barrier, inc=1, device_id=spot_of(k), device_id_type=pl.DeviceIdType.MESH
    ))

    def loop(size, body, start):
        unroll = next(u for u in (4, 3, 2, 1) if size % u == 0)

        def several(i, carry):
            for j in range(unroll):
                carry = body(i * unroll + j, carry)
            return carry

        return lax.fori_loop(0, size // unroll, several, start)

    lane = lax.broadcasted_iota(jnp.int32, (nx, ny), 1)
    row = lax.broadcasted_iota(jnp.int32, (nx, ny), 0)

    def up(axis, own, ghost):
        at = (row if axis == 0 else lane) == 0
        return pltpu.roll(jnp.where(at, ghost, own), own.shape[axis] - 1, axis)

    def down(axis, own, ghost):
        size = own.shape[axis]
        at = (row if axis == 0 else lane) == size - 1
        return pltpu.roll(jnp.where(at, ghost, own), 1, axis)

    slot = [0]

    class Exchange:
        def __init__(self, copies):
            self.copies = []
            for axis, step, src, dst in copies:
                if count[axis] == 1:
                    self.copies.append((axis, dst, None, None, None))
                    continue
                copy = pltpu.make_async_remote_copy(
                    src_ref=src, dst_ref=dst, send_sem=send_sem.at[slot[0]], recv_sem=recv_sem.at[slot[0]],
                    device_id={axis: index[axis] + step}, device_id_type=pl.DeviceIdType.MESH,
                )
                slot[0] += 1
                low, high = index[axis] > 0, index[axis] < count[axis] - 1
                sends, receives = (high, low) if step > 0 else (low, high)
                self.copies.append((axis, dst, copy, sends, receives))

        def clear(self):
            for _, dst, copy, _, receives in self.copies:
                def zero(dst=dst):
                    dst[...] = jnp.zeros(dst.shape, dst.dtype)
                if copy is None:
                    zero()
                else:
                    pl.when(jnp.logical_not(receives))(zero)

        def start(self, axes=AXES):
            for axis, _, copy, sends, _ in self.copies:
                if copy is not None and axis in axes:
                    pl.when(sends)(copy.start)

        def wait(self, axes=AXES):
            for axis, _, copy, _, receives in self.copies:
                if copy is not None and axis in axes:
                    pl.when(receives)(copy.wait_recv)

        def finish(self):
            for _, _, copy, sends, _ in self.copies:
                if copy is not None:
                    pl.when(sends)(copy.wait_send)

    def rows_of(src, dst, first, depth, skip=0):
        hi, lo = pl.ds(nx - depth - skip, depth), pl.ds(skip, depth)
        lead = (slice(None),) * (len(dst.shape) - 3)
        return [
            ("gx", 1, src.at[lead + (pl.ds(first, nz), hi)], dst.at[lead + (slice(None), hi)]),
            ("gx", -1, src.at[lead + (pl.ds(first, nz), lo)], dst.at[lead + (slice(None), lo)]),
        ]

    def planes_of(src, first, depth, pick=slice(None), lead=True):
        def at(start):
            return src.at[pick, pl.ds(start, depth)] if lead else src.at[pl.ds(start, depth)]
        return [
            ("gz", 1, at(first + nz - depth), at(first - depth)),
            ("gz", -1, at(first), at(first + nz)),
        ]

    def pack(dst, fields):
        for k in range(dst.shape[0]):
            acc = jnp.zeros((nx, ny), jnp.float32)
            for j, field in enumerate(fields[k * per:(k + 1) * per]):
                for z in range(nz):
                    spot = j * nz + z
                    moved = pltpu.roll(field(z).astype(jnp.float32), (group * spot + 2) % ny, 1)
                    acc = jnp.where(lane // group == spot, moved, acc)
            dst[k] = acc

    def merge(low, high):
        for k in range(low.shape[0]):
            low[k] = jnp.where(lax.rem(lane, group) < 2, low[k], high[k])

    def side(merged, f, z):
        spot = f % per * nz + z
        return pltpu.roll(merged[f // per], lax.rem(2 * ny - group * spot - 2, ny), 1)

    def y_copies(packed, low, high):
        return [("gy", 1, packed, low), ("gy", -1, packed, high)]

    first = Exchange(
        rows_of(se0, xs0, 2, 1) + rows_of(ve0.at[0], xv0, 0, 1, 1)
        + rows_of(ge, xg, 2, 1) + rows_of(we.at[0], xw.at[0], 2, 1)
        + planes_of(se0, 2, 2) + planes_of(ge, 2, 2, lead=False) + planes_of(we, 2, 2)
        + y_copies(yp1, yl1, yu1)
    )
    later = Exchange(rows_of(we.at[1], xw.at[1], 2, 1))
    second = Exchange(
        rows_of(se1.at[pl.ds(0, 2)], xs1, 2, 1) + rows_of(q1.at[0], xq.at[0], 0, 1, 1)
        + rows_of(q1.at[1], xq.at[1], 0, 1) + planes_of(se1, 2, 1) + y_copies(yp2, yl2, yu2)
    )
    third = Exchange(
        rows_of(lam.at[1], xl.at[1], 1, 2) + rows_of(lam.at[0], xl.at[0], 1, 1)
        + planes_of(lam, 1, 1) + y_copies(yp3, yl3, yu3)
    )
    fourth = Exchange(
        rows_of(xe, xm, 0, 1) + planes_of(zm, 1, 1) + y_copies(yp4, yl4, yu4)
    )
    exchanges = (first, later, second, third, fourth)
    for exchange in exchanges:
        exchange.clear()
    for copy in loads:
        copy.wait()
    for z in range(nz):
        ve0[0, z] = se0[1, z + 2] / (1.0 + se0[0, z + 2])
    pack(yp1, [lambda z, f=f: se0[f, z + 2] for f in range(5)] + [lambda z: ge[z + 2], lambda z: we[0, z + 2]])

    cells_row = pr[...] // ny
    cells_col = lax.rem(pr[...], ny)
    probes = pr.shape[1]
    hot_a[...] = (lax.broadcasted_iota(jnp.int32, (nz * nx, probes), 0) == cells_row).astype(jnp.float32)
    hot_b[...] = (lax.broadcasted_iota(jnp.int32, (ny, probes), 0) == cells_col).astype(jnp.float32)

    pl.semaphore_wait(barrier, total - 1)
    first.start()

    last_dims = (((1,), (1,)), ((), ()))
    cnt[...] = lax.dot_general(hot_a[...], hot_b[...], last_dims, precision=HI, preferred_element_type=jnp.float32)
    sob[...] = lax.dot_general(
        hot_a[...], hot_b[...] * ob[...], last_dims, precision=HI, preferred_element_type=jnp.float32
    )

    def prim(u):
        rho = 1.0 + u[0]
        inv = 1.0 / rho
        vels = [u[1] * inv, u[2] * inv, u[3] * inv]
        internal = u[4] * inv - 0.5 * (vels[0] * vels[0] + vels[1] * vels[1] + vels[2] * vels[2])
        return rho, inv, vels, internal

    def press(u, gamma, rho, internal):
        return BULK * (u[0] + SLOPE * u[0] * u[0]) + gamma * rho * internal

    def flux(a, u, speed, pressure, rho, s, slope):
        squeeze = jnp.minimum(slope, 0.0)
        t = pressure + s * QUAD * rho * squeeze * squeeze
        f = [u[1 + a]] + [u[1 + b] * speed for b in range(3)] + [(u[4] + t) * speed]
        f[1 + a] = f[1 + a] + t
        a_side = [0.5 * f[c] - 0.5 * SIGNAL * u[c] for c in range(5)]
        b_side = [0.5 * f[c] + 0.5 * SIGNAL * u[c] for c in range(5)]
        return a_side, b_side

    edge = (row == 0) | (row == nx - 1)

    def paired(a, axis, u, pv, uh, gh, sh, s, far=None):
        rho, _, vels, _, p = pv
        rho_h, _, vels_h, e_h = prim(uh)
        p_h = press(uh, gh, rho_h, e_h)
        v, v_h = vels[a], vels_h[a]
        if far is not None:
            v_h = jnp.where(edge, v_h, far)
        slope = 0.5 * (up(axis, v, v_h) - down(axis, v, v_h))
        slope_h = 0.5 * (up(axis, v_h, v) - down(axis, v_h, v))
        ao, bo = flux(a, u, v, p, rho, s, slope)
        ah, bh = flux(a, uh, v_h, p_h, rho_h, sh, slope_h)
        return [up(axis, ao[c], ah[c]) - down(axis, bo[c], bh[c]) for c in range(5)], v_h

    first.wait(("gz",))

    def z_pass(e, carry):
        u = [se0[c, e + 1] for c in range(5)]
        rho, _, vels, internal = prim(u)
        p = press(u, ge[e + 1], rho, internal)
        s = we[0, e + 1].astype(jnp.float32)
        above = se0[3, e + 2] / (1.0 + se0[0, e + 2])
        below = se0[3, e] / (1.0 + se0[0, e])
        a_side, b_side = flux(2, u, vels[2], p, rho, s, 0.5 * (above - below))
        for c in range(5):
            az[c, e] = a_side[c]
            bz[c, e] = b_side[c]
        return carry

    loop(nz + 2, z_pass, 0)
    first.wait(("gy",))
    merge(yl1, yu1)

    def step_one(z, carry):
        u = [se0[c, z + 2] for c in range(5)]
        rho, inv, vels, internal = prim(u)
        energy = rho * internal
        p = press(u, ge[z + 2], rho, internal)
        s = we[0, z + 2].astype(jnp.float32)
        pv = (rho, inv, vels, internal, p)
        dy = paired(1, 1, u, pv, [side(yl1, c, z) for c in range(5)], side(yl1, 5, z), side(yl1, 6, z), s)[0]
        for c in range(5):
            change = dy[c] + az[c, z + 2] - bz[c, z] + 3.0 * SIGNAL * u[c]
            se1[c, z + 2] = u[c] - DT * change
        en0[z] = energy
        for a in range(1, 3):
            ve0[a, z] = vels[a]
        q1[1, z] = p
        return carry

    loop(nz, step_one, 0)
    first.wait(("gx",))
    later.start()

    def step_one_x(z, carry):
        u = [se0[c, z + 2] for c in range(5)]
        rho = 1.0 + u[0]
        s = we[0, z + 2].astype(jnp.float32)
        pv = (rho, None, [ve0[0, z]], None, q1[1, z])
        dx, vh0[z] = paired(
            0, 0, u, pv, [xs0[c, z] for c in range(5)], xg[z], xw[0, z].astype(jnp.float32), s, xv0[z]
        )
        new = [se1[c, z + 2] - DT * dx[c] for c in range(5)]
        rho, _, vels, internal = prim(new)
        for c in range(5):
            se1[c, z + 2] = new[c]
        q1[0, z] = vels[0]
        q1[1, z] = press(new, ge[z + 2], rho, internal)
        return carry

    loop(nz, step_one_x, 0)
    second.start(("gx", "gz"))
    pack(yp2, [lambda z, f=f: se1[f, z + 2] for f in range(3)])
    second.start(("gy",))
    second.wait(("gz", "gy"))
    merge(yl2, yu2)
    second.wait(("gx",))
    later.wait()

    def step_two(z, carry):
        u = [se1[c, z + 2] for c in range(4)]
        s = we[1, z + 2].astype(jnp.float32) * QUAD * (1.0 + u[0])
        sh = xw[1, z].astype(jnp.float32) * QUAD * (1.0 + xs1[0, z])
        v, v_h = q1[0, z], jnp.where(edge, xs1[1, z] / (1.0 + xs1[0, z]), xq[0, z])
        squeeze = jnp.minimum(0.5 * (up(0, v, v_h) - down(0, v, v_h)), 0.0)
        squeeze_h = jnp.minimum(0.5 * (up(0, v_h, v) - down(0, v_h, v)), 0.0)
        kap[z] = 2.0 * s * squeeze
        kah[z] = 2.0 * sh * squeeze_h

        def along(r, mx, speed, t):
            f = [0.5 * mx, 0.5 * (mx * speed + t)]
            d = [0.5 * SIGNAL * r, 0.5 * SIGNAL * mx]
            return [f[0] - d[0], f[1] - d[1]], [f[0] + d[0], f[1] + d[1]]

        ax, bx = along(u[0], u[1], v, q1[1, z] + s * squeeze * squeeze)
        axh, bxh = along(xs1[0, z], xs1[1, z], v_h, xq[1, z] + sh * squeeze_h * squeeze_h)
        dx = [up(0, ax[c], axh[c]) - down(0, bx[c], bxh[c]) for c in range(2)]

        def simple(r, mx, ma):
            f = [0.5 * ma, 0.5 * mx * (ma / (1.0 + r))]
            d = [0.5 * SIGNAL * r, 0.5 * SIGNAL * mx]
            return [f[0] - d[0], f[1] - d[1]], [f[0] + d[0], f[1] + d[1]]

        ao, bo = simple(u[0], u[1], u[2])
        ah, bh = simple(side(yl2, 0, z), side(yl2, 1, z), side(yl2, 2, z))
        above = simple(se1[0, z + 3], se1[1, z + 3], se1[3, z + 3])[0]
        below = simple(se1[0, z + 1], se1[1, z + 1], se1[3, z + 1])[1]
        new = []
        for c in range(2):
            change = dx[c] + up(1, ao[c], ah[c]) - down(1, bo[c], bh[c]) + above[c] - below[c] + 3.0 * SIGNAL * u[c]
            new.append(u[c] - DT * change)
        inv2 = 1.0 / (1.0 + new[0])
        v = new[1] * inv2
        at = pl.ds(pl.multiple_of(z * nx, nx), nx)
        vel[at, :] = v
        w = 2.0 * (cnt[at, :] * v - sob[at, :]) * inv2
        lam[0, z + 1] = -w * v
        lam[1, z + 1] = w
        return carry

    loop(nz, step_two, 0)

    third.start(("gx", "gz"))
    pack(yp3, [lambda z, f=f: lam[f, z + 1] for f in range(2)])
    third.start(("gy",))

    picked = jnp.dot(vel[...], hot_b[...], precision=HI, preferred_element_type=jnp.float32)
    speed = jnp.sum(picked * hot_a[...], axis=0, keepdims=True)
    miss = (speed - ob[...]) * (speed - ob[...])
    miss = sum(miss[:, k * ny:(k + 1) * ny] for k in range(probes // ny))

    third.wait()
    merge(yl3, yu3)
    half = 0.5 * DT

    def adjoint_two(z, carry):
        u = [se1[c, z + 2] for c in range(5)]
        rho, inv, vels, internal = prim(u)
        gamma = ge[z + 2]
        l0, l1 = lam[0, z + 1], lam[1, z + 1]
        x0, x1 = xl[0, z], xl[1, z]
        y0, y1 = side(yl3, 0, z), side(yl3, 1, z)
        ups0 = [up(0, l0, x0), up(1, l0, y0), lam[0, z + 2]]
        dns0 = [down(0, l0, x0), down(1, l0, y0), lam[0, z]]
        ups1 = [up(0, l1, x1), up(1, l1, y1), lam[1, z + 2]]
        dns1 = [down(0, l1, x1), down(1, l1, y1), lam[1, z]]
        p0 = [half * (ups0[a] - dns0[a]) for a in range(3)]
        p1 = [half * (ups1[a] - dns1[a]) for a in range(3)]
        ghost = half * (up(0, x1, l1) - down(0, x1, l1))
        sigma = kap[z] * p1[0]
        sigma_h = kah[z] * ghost
        around = ups1[0] + dns1[0] + ups1[1] + dns1[1] + ups1[2] + dns1[2]
        pi = p1[0]
        eps = pi * gamma * rho
        cots = [p1[a] * u[1] - eps * vels[a] for a in range(3)]
        cots[0] = cots[0] + 0.5 * (down(0, sigma, sigma_h) - up(0, sigma, sigma_h))
        weight = 0.5 * DT * SIGNAL
        zm[0, z + 1] = p0[2] + cots[2] * inv
        zm[1, z + 1] = pi * gamma
        ze[0, z] = (
            l1 * (1.0 - 6.0 * weight) + weight * around + p0[0]
            + p1[0] * vels[0] + p1[1] * vels[1] + p1[2] * vels[2] + cots[0] * inv
        )
        ze[1, z] = pi * gamma
        v0, g0 = ve0[0, z], vh0[z]
        xe[z] = ze[0, z] + pi * gamma * jnp.where(row == 0, down(0, v0, g0), up(0, v0, g0))
        ze[2, z] = p0[1] + cots[1] * inv
        gam2[z] = pi * rho * internal
        return carry

    loop(nz, adjoint_two, 0)

    fourth.start(("gx", "gz"))
    pack(yp4, [lambda z: ze[2, z], lambda z: ze[1, z]])
    fourth.start(("gy",))
    fourth.wait()
    merge(yl4, yu4)

    def adjoint_one(z, acc):
        vels = [ve0[a, z] for a in range(3)]
        mx, en, my = ze[0, z], ze[1, z], ze[2, z]
        xa = xm[z]
        none = jnp.zeros_like(xa)
        ya, ye = side(yl4, 0, z), side(yl4, 1, z)
        pi = (
            up(0, mx, xa) - down(0, mx, xa) + up(1, my, ya) - down(1, my, ya) + zm[0, z + 2] - zm[0, z]
            + vels[0] * (up(0, en, none) - down(0, en, none))
            + vels[1] * (up(1, en, ye) - down(1, en, ye))
            + vels[2] * (zm[1, z + 2] - zm[1, z])
        )
        g = gam2[z] + half * pi * en0[z]
        grad[z] = g
        return acc + g * g

    square = loop(nz, adjoint_one, jnp.zeros((nx, ny), jnp.float32))
    mine[pl.ds(0, 1), :] = jnp.sum(square, axis=0, keepdims=True)
    mine[pl.ds(1, 1), :] = miss
    def all_copy(k, slot_at):
        return pltpu.make_async_remote_copy(
            src_ref=mine, dst_ref=ar.at[slot_at], send_sem=all_send.at[k], recv_sem=all_recv.at[slot_at],
            device_id=spot_of(k), device_id_type=pl.DeviceIdType.MESH,
        )

    each_peer(lambda k: all_copy(k, me).start())
    ar[me] = mine[...]
    out = pltpu.make_async_copy(grad, grad_out, local_sem.at[0])
    out.start()
    for exchange in exchanges:
        exchange.finish()
    each_peer(lambda k: all_copy(k, flat(spot_of(k))).wait_recv())
    sums = jnp.sum(ar[...], axis=0)
    cells = total * nz * nx * ny
    mean = jnp.sum(sums[0:1, :], axis=1, keepdims=True) / cells
    mis_out[...] = jnp.sum(sums[1:2, :], axis=1, keepdims=True) / (total * probes)
    scale_out[...] = 1.0 / jnp.sqrt(mean + EPS)
    each_peer(lambda k: all_copy(k, me).wait_send())
    out.wait()


def local(sizes, checkpoint, gruneisen, switch, probes, observed):
    nz, nx, ny = gruneisen.shape
    count = probes.shape[0]
    total = math.prod(sizes)
    f32 = jnp.float32

    def vm(*shape, dtype=f32):
        return pltpu.VMEM(shape, dtype)

    per = ny // (4 * nz)
    packs = []
    for fields in (7, 3, 2, 2):
        packs += [vm(-(-fields // per), nx, ny)] * 3
    any_spec = pl.BlockSpec(memory_space=pl.ANY)
    vmem = pl.BlockSpec(memory_space=pltpu.VMEM)
    gradient, misfit, scale = pl.pallas_call(
        functools.partial(kernel, sizes),
        out_shape=(jax.ShapeDtypeStruct((nz, nx, ny), f32),) + (jax.ShapeDtypeStruct((1, 1), f32),) * 2,
        in_specs=[pl.BlockSpec(memory_space=pltpu.HBM)] * 5,
        out_specs=(any_spec, vmem, vmem),
        scratch_shapes=[
            vm(5, nz + 4, nx, ny), vm(5, nz + 4, nx, ny), vm(nz + 4, nx, ny), vm(2, nz + 4, nx, ny, dtype=jnp.int32),
            vm(5, nz, nx, ny), vm(nz, nx, ny), vm(2, nz, nx, ny, dtype=jnp.int32),
            vm(2, nz, nx, ny), vm(2, nz, nx, ny), vm(2, nz, nx, ny), vm(nz, nx, ny), vm(nz, nx, ny), vm(nz, nx, ny),
            vm(1, count, dtype=jnp.int32), vm(1, count), vm(nz, nx, ny), vm(3, nz, nx, ny),
            vm(2, nz, nx, ny), vm(nz, nx, ny),
            vm(3, nz, nx, ny), vm(5, nz + 2, nx, ny), vm(5, nz + 2, nx, ny), vm(2, nz + 2, nx, ny),
            vm(nz, nx, ny), vm(nz, nx, ny), vm(nz, nx, ny), vm(2, nz + 2, nx, ny),
            *packs,
            vm(nz * nx, ny), vm(nz * nx, ny), vm(nz * nx, ny), vm(nz * nx, count), vm(ny, count), vm(nz, nx, ny),
            vm(2, ny), vm(total, 2, ny),
            pltpu.SemaphoreType.DMA((5,)), pltpu.SemaphoreType.DMA((48,)), pltpu.SemaphoreType.DMA((48,)),
            pltpu.SemaphoreType.DMA((total,)), pltpu.SemaphoreType.DMA((total,)),
        ],
        compiler_params=pltpu.CompilerParams(collective_id=0, has_side_effects=True),
        name="adjoint",
    )(checkpoint, gruneisen, switch, probes.reshape(1, count), observed.reshape(1, count))
    return gradient * scale.reshape(()), misfit.reshape(())


def solution(mesh):
    sizes = tuple(mesh.shape[a] for a in AXES)
    placed = (P(None, "gz", "gx", "gy"), P("gz", "gx", "gy"), P(None, "gz", "gx", "gy"), P(AXES), P(AXES))
    return jax.shard_map(
        functools.partial(local, sizes), mesh=mesh, in_specs=placed,
        out_specs=(P("gz", "gx", "gy"), P()), check_vma=False,
    )
```

profile of v0, /device:TPU:0, one launch (start us, length us, event | category | flops | bytes accessed | tf_op | source)
XLA Modules:
  0.0 34.3 jit_solution(2058742395469684315)
XLA Ops:
  0.6 29.8 %adjoint.1 = (f32[16,8,128]{2,1,0:T(8,128)}, f32[1,1]{1,0:T(1,128)}, f32[1,1]{1,0:T(1,128)}) custom-call(f32[5,16,8,128]{3,2,1,0:T(8,128)} %st.1, f32[16,8,128]{2,1,0:T(8,128)} %ga.1, s32[2,16,8,128]{3,2,1,0:T(8,128)} %sw.1, s32[1,256]{1,0:T(1,128)} %bitcast.4, f32[1,256]{1,0:T(1,128)} %bitcast.5), custom_call_target="tpu_custom_call" | custom-call | tf_op jit(solution)/shard_map/adjoint/pallas_call | solution.py:468
  30.5 2.0 %broadcast_multiply_fusion = f32[16,8,128]{2,1,0:T(8,128)} fusion(f32[16,8,128]{2,1,0:T(8,128)} %get-tuple-element.5, f32[]{:T(128)} %bitcast.2), kind=kLoop, calls=%fused_computation | loop fusion | flops 16384 | bytes 131076 | tf_op jit(solution)/shard_map/mul | solution.py:490
where the time goes:
time: 34.5 us; the launch traced here: 34.3 us
  Pallas kernels  29.8 us (86%)
  between operations  2.39 us (7%)
  other arithmetic  2.03 us (6%)
    pallas_call x1, Pallas kernels, local(): pl.pallas_call(functools.partial(kernel, sizes), out_shape=(jax.ShapeDtyp...  29.8 us
    mul x1, other arithmetic, local(): return (gradient * scale.reshape(()), misfit.reshape(()))  2.03 us

commit v1 on v0

--- a/solution.py
+++ b/solution.py
@@ -19,7 +19,7 @@
 
 
 def kernel(
-    sizes, st, ga, sw, pr_in, ob_in, grad_out, mis_out, scale_out,
+    sizes, st, ga, sw, pr_in, ob_in, result,
     se0, se1, ge, we, xs0, xg, xw, xs1, xq, q1, xv0, vh0, xe, pr, ob, en0, ve0, xl, xm, ze, az, bz, zm, kap, kah, gam2, lam,
     yp1, yl1, yu1, yp2, yl2, yu2, yp3, yl3, yu3, yp4, yl4, yu4, cnt, sob, vel, hot_a, hot_b, grad,
     mine, ar, local_sem, send_sem, recv_sem, all_send, all_recv,
@@ -436,18 +436,23 @@
 
     each_peer(lambda k: all_copy(k, me).start())
     ar[me] = mine[...]
-    out = pltpu.make_async_copy(grad, grad_out, local_sem.at[0])
-    out.start()
     for exchange in exchanges:
         exchange.finish()
     each_peer(lambda k: all_copy(k, flat(spot_of(k))).wait_recv())
     sums = jnp.sum(ar[...], axis=0)
     cells = total * nz * nx * ny
     mean = jnp.sum(sums[0:1, :], axis=1, keepdims=True) / cells
-    mis_out[...] = jnp.sum(sums[1:2, :], axis=1, keepdims=True) / (total * probes)
-    scale_out[...] = 1.0 / jnp.sqrt(mean + EPS)
+    misfit = jnp.sum(sums[1:2, :], axis=1, keepdims=True) / (total * probes)
+    scale = 1.0 / jnp.sqrt(mean + EPS)
+    result[pl.ds(0, nz)] = grad[...] * jnp.broadcast_to(scale, (nx, ny))
+    result[nz] = jnp.broadcast_to(misfit, (nx, ny))
     each_peer(lambda k: all_copy(k, me).wait_send())
-    out.wait()
+
+
+def store(result, direction, misfit):
+    nz = direction.shape[0]
+    direction[...] = result[pl.ds(0, nz)]
+    misfit[0, 0] = result[nz, 0:1, 0:1][0, 0]
 
 
 def local(sizes, checkpoint, gruneisen, switch, probes, observed):
@@ -463,13 +468,14 @@
     packs = []
     for fields in (7, 3, 2, 2):
         packs += [vm(-(-fields // per), nx, ny)] * 3
-    any_spec = pl.BlockSpec(memory_space=pl.ANY)
     vmem = pl.BlockSpec(memory_space=pltpu.VMEM)
-    gradient, misfit, scale = pl.pallas_call(
+    smem = pl.BlockSpec(memory_space=pltpu.SMEM)
+    inputs = (checkpoint, gruneisen, switch, probes.reshape(1, count), observed.reshape(1, count))
+    result = pl.pallas_call(
         functools.partial(kernel, sizes),
-        out_shape=(jax.ShapeDtypeStruct((nz, nx, ny), f32),) + (jax.ShapeDtypeStruct((1, 1), f32),) * 2,
+        out_shape=jax.ShapeDtypeStruct((nz + 1, nx, ny), f32),
         in_specs=[pl.BlockSpec(memory_space=pltpu.HBM)] * 5,
-        out_specs=(any_spec, vmem, vmem),
+        out_specs=vmem,
         scratch_shapes=[
             vm(5, nz + 4, nx, ny), vm(5, nz + 4, nx, ny), vm(nz + 4, nx, ny), vm(2, nz + 4, nx, ny, dtype=jnp.int32),
             vm(5, nz, nx, ny), vm(nz, nx, ny), vm(2, nz, nx, ny, dtype=jnp.int32),
@@ -484,10 +490,18 @@
             pltpu.SemaphoreType.DMA((5,)), pltpu.SemaphoreType.DMA((48,)), pltpu.SemaphoreType.DMA((48,)),
             pltpu.SemaphoreType.DMA((total,)), pltpu.SemaphoreType.DMA((total,)),
         ],
-        compiler_params=pltpu.CompilerParams(collective_id=0, has_side_effects=True),
+        compiler_params=pltpu.CompilerParams(collective_id=0, has_side_effects=True, vmem_limit_bytes=32 << 20),
         name="adjoint",
-    )(checkpoint, gruneisen, switch, probes.reshape(1, count), observed.reshape(1, count))
-    return gradient * scale.reshape(()), misfit.reshape(())
+    )(*(pltpu.with_memory_space_constraint(a, pltpu.HBM) for a in inputs))
+    direction, misfit = pl.pallas_call(
+        store,
+        out_shape=(jax.ShapeDtypeStruct((nz, nx, ny), f32), jax.ShapeDtypeStruct((1, 1), f32)),
+        in_specs=[vmem],
+        out_specs=(vmem, smem),
+        compiler_params=pltpu.CompilerParams(vmem_limit_bytes=1 << 20),
+        name="store",
+    )(result)
+    return direction, misfit.reshape(())
 
 
 def solution(mesh):

time: 34.5 us -> 30.7 us (0.89)
  other arithmetic: 2.03 us -> 0 us
  between operations: 2.39 us -> 0.64 us
    mul x1 -> x0, other arithmetic: 2.03 us -> none  [local(): return (gradient * scale.reshape(()), misfit.reshape(()))]
    pallas_call x1 -> x2, Pallas kernels: 29.8 us -> 30 us  [the longest x1 29.3 us: local(): pl.pallas_call(functools.partial(kernel, sizes), out_shape=jax.ShapeDtype...]
where the time goes in v1:
time: 30.7 us; the launch traced here: 30.6 us
  Pallas kernels  30 us (98%)
  between operations  0.64 us (2%)
    pallas_call x1, Pallas kernels, local(): pl.pallas_call(functools.partial(kernel, sizes), out_shape=jax.ShapeDtype...  29.3 us
    pallas_call x1, Pallas kernels, local(): pl.pallas_call(store, out_shape=(jax.ShapeDtypeStruct((nz, nx, ny), f32),...  0.64 us

profile of v1, /device:TPU:0, one launch (start us, length us, event | category | flops | bytes accessed | tf_op | source)
XLA Modules:
  0.0 30.6 jit_solution(17505345521533817534)
XLA Ops:
  0.6 29.3 %adjoint.1.result = f32[17,8,128]{2,1,0:T(8,128)S(1)} custom-call(f32[5,16,8,128]{3,2,1,0:T(8,128)} %st.1, f32[16,8,128]{2,1,0:T(8,128)} %ga.1, s32[2,16,8,128]{3,2,1,0:T(8,128)} %sw.1, s32[1,256]{1,0:T(1,128)} %bitcast.3, f32[1,256]{1,0:T(1,128)} %bitcast.4), custom_call_target="tpu_custom_call" | custom-call | tf_op jit(solution)/shard_map/adjoint/pallas_call | solution.py:474
  30.0 0.6 %store.1 = (f32[16,8,128]{2,1,0:T(8,128)}, f32[1,1]{1,0:T(1,128)}) custom-call(f32[17,8,128]{2,1,0:T(8,128)S(1)} %adjoint.1.result), custom_call_target="tpu_custom_call" | custom-call | tf_op jit(solution)/shard_map/store/pallas_call | solution.py:496

commit v2 on v1

--- a/solution.py
+++ b/solution.py
@@ -20,8 +20,9 @@
 
 def kernel(
     sizes, st, ga, sw, pr_in, ob_in, result,
-    se0, se1, ge, we, xs0, xg, xw, xs1, xq, q1, xv0, vh0, xe, pr, ob, en0, ve0, xl, xm, ze, az, bz, zm, kap, kah, gam2, lam,
-    yp1, yl1, yu1, yp2, yl2, yu2, yp3, yl3, yu3, yp4, yl4, yu4, cnt, sob, vel, hot_a, hot_b, grad,
+    se0, se1, ge, we, xs0, xg, xw, xs1, xt1, xq, q1, xv0, vh0, pr, ob, en0, ve0, xl, xk, xa, ze, az, bz, zm, kap, kah, sig, gam2,
+    lam, yr,
+    yp1, yl1, yu1, yp2, yl2, yu2, yp3, yl3, yu3, el3, eu3, cnt, sob, vel, hot_a, hot_b, grad,
     mine, ar, local_sem, send_sem, recv_sem, all_send, all_recv,
 ):
     nz, nx, ny = ga.shape
@@ -95,18 +96,20 @@
     class Exchange:
         def __init__(self, copies):
             self.copies = []
-            for axis, step, src, dst in copies:
-                if count[axis] == 1:
-                    self.copies.append((axis, dst, None, None, None))
+            for name, steps, src, dst in copies:
+                if any(count[a] == 1 for a in steps):
+                    self.copies.append((name, dst, None, None, None))
                     continue
                 copy = pltpu.make_async_remote_copy(
                     src_ref=src, dst_ref=dst, send_sem=send_sem.at[slot[0]], recv_sem=recv_sem.at[slot[0]],
-                    device_id={axis: index[axis] + step}, device_id_type=pl.DeviceIdType.MESH,
+                    device_id={a: index[a] + step for a, step in steps.items()}, device_id_type=pl.DeviceIdType.MESH,
                 )
                 slot[0] += 1
-                low, high = index[axis] > 0, index[axis] < count[axis] - 1
-                sends, receives = (high, low) if step > 0 else (low, high)
-                self.copies.append((axis, dst, copy, sends, receives))
+                low = {a: index[a] > 0 for a in steps}
+                high = {a: index[a] < count[a] - 1 for a in steps}
+                sends = functools.reduce(jnp.logical_and, [high[a] if step > 0 else low[a] for a, step in steps.items()])
+                receives = functools.reduce(jnp.logical_and, [low[a] if step > 0 else high[a] for a, step in steps.items()])
+                self.copies.append((name, dst, copy, sends, receives))
 
         def clear(self):
             for _, dst, copy, _, receives in self.copies:
@@ -117,12 +120,12 @@
                 else:
                     pl.when(jnp.logical_not(receives))(zero)
 
-        def start(self, axes=AXES):
+        def start(self, axes=AXES + ("edge",)):
             for axis, _, copy, sends, _ in self.copies:
                 if copy is not None and axis in axes:
                     pl.when(sends)(copy.start)
 
-        def wait(self, axes=AXES):
+        def wait(self, axes=AXES + ("edge",)):
             for axis, _, copy, _, receives in self.copies:
                 if copy is not None and axis in axes:
                     pl.when(receives)(copy.wait_recv)
@@ -132,20 +135,20 @@
                 if copy is not None:
                     pl.when(sends)(copy.wait_send)
 
-    def rows_of(src, dst, first, depth, skip=0):
+    def rows_of(src, dst, first, depth, skip=0, start=0):
         hi, lo = pl.ds(nx - depth - skip, depth), pl.ds(skip, depth)
         lead = (slice(None),) * (len(dst.shape) - 3)
         return [
-            ("gx", 1, src.at[lead + (pl.ds(first, nz), hi)], dst.at[lead + (slice(None), hi)]),
-            ("gx", -1, src.at[lead + (pl.ds(first, nz), lo)], dst.at[lead + (slice(None), lo)]),
+            ("gx", {"gx": 1}, src.at[lead + (pl.ds(first, nz), hi)], dst.at[lead + (pl.ds(start, nz), hi)]),
+            ("gx", {"gx": -1}, src.at[lead + (pl.ds(first, nz), lo)], dst.at[lead + (pl.ds(start, nz), lo)]),
         ]
 
     def planes_of(src, first, depth, pick=slice(None), lead=True):
         def at(start):
             return src.at[pick, pl.ds(start, depth)] if lead else src.at[pl.ds(start, depth)]
         return [
-            ("gz", 1, at(first + nz - depth), at(first - depth)),
-            ("gz", -1, at(first), at(first + nz)),
+            ("gz", {"gz": 1}, at(first + nz - depth), at(first - depth)),
+            ("gz", {"gz": -1}, at(first), at(first + nz)),
         ]
 
     def pack(dst, fields):
@@ -167,7 +170,16 @@
         return pltpu.roll(merged[f // per], lax.rem(2 * ny - group * spot - 2, ny), 1)
 
     def y_copies(packed, low, high):
-        return [("gy", 1, packed, low), ("gy", -1, packed, high)]
+        return [("gy", {"gy": 1}, packed, low), ("gy", {"gy": -1}, packed, high)]
+
+    def edge_copies():
+        copies = []
+        for sx, line in ((1, pl.ds(nx - 1, 1)), (-1, pl.ds(0, 1))):
+            for sy, dst in ((1, el3), (-1, eu3)):
+                copies.append(("edge", {"gx": sx, "gy": sy}, yp3.at[:, line], dst.at[:, line]))
+            for sz, src, dst in ((1, nz + 1, 0), (-1, 2, nz + 1)):
+                copies.append(("edge", {"gx": sx, "gz": sz}, lam.at[1, src, line], xl.at[1, dst, line]))
+        return copies
 
     first = Exchange(
         rows_of(se0, xs0, 2, 1) + rows_of(ve0.at[0], xv0, 0, 1, 1)
@@ -180,14 +192,12 @@
         rows_of(se1.at[pl.ds(0, 2)], xs1, 2, 1) + rows_of(q1.at[0], xq.at[0], 0, 1, 1)
         + rows_of(q1.at[1], xq.at[1], 0, 1) + planes_of(se1, 2, 1) + y_copies(yp2, yl2, yu2)
     )
+    extra = Exchange(rows_of(se1.at[pl.ds(2, 2)], xt1, 2, 1))
     third = Exchange(
-        rows_of(lam.at[1], xl.at[1], 1, 2) + rows_of(lam.at[0], xl.at[0], 1, 1)
-        + planes_of(lam, 1, 1) + y_copies(yp3, yl3, yu3)
+        rows_of(lam, xl, 2, 2, 0, 1) + rows_of(sig, xk, 0, 1, 1)
+        + planes_of(lam, 2, 2) + y_copies(yp3, yl3, yu3) + edge_copies()
     )
-    fourth = Exchange(
-        rows_of(xe, xm, 0, 1) + planes_of(zm, 1, 1) + y_copies(yp4, yl4, yu4)
-    )
-    exchanges = (first, later, second, third, fourth)
+    exchanges = (first, later, second, extra, third)
     for exchange in exchanges:
         exchange.clear()
     for copy in loads:
@@ -305,6 +315,7 @@
     second.start(("gx", "gz"))
     pack(yp2, [lambda z, f=f: se1[f, z + 2] for f in range(3)])
     second.start(("gy",))
+    extra.start()
     second.wait(("gz", "gy"))
     merge(yl2, yu2)
     second.wait(("gx",))
@@ -347,39 +358,89 @@
         at = pl.ds(pl.multiple_of(z * nx, nx), nx)
         vel[at, :] = v
         w = 2.0 * (cnt[at, :] * v - sob[at, :]) * inv2
-        lam[0, z + 1] = -w * v
-        lam[1, z + 1] = w
+        lam[0, z + 2] = -w * v
+        lam[1, z + 2] = w
+        sig[z] = s * squeeze * DT * (pltpu.roll(w, nx - 1, 0) - pltpu.roll(w, 1, 0))
         return carry
 
     loop(nz, step_two, 0)
 
     third.start(("gx", "gz"))
-    pack(yp3, [lambda z, f=f: lam[f, z + 1] for f in range(2)])
-    third.start(("gy",))
+    pack(yp3, [lambda z, f=f: lam[f, z + 2] for f in range(2)])
+    third.start(("gy", "edge"))
 
     picked = jnp.dot(vel[...], hot_b[...], precision=HI, preferred_element_type=jnp.float32)
     speed = jnp.sum(picked * hot_a[...], axis=0, keepdims=True)
     miss = (speed - ob[...]) * (speed - ob[...])
     miss = sum(miss[:, k * ny:(k + 1) * ny] for k in range(probes // ny))
 
+    half = 0.5 * DT
+    weight = 0.5 * DT * SIGNAL
+    first_row, last_row = index["gx"] > 0, index["gx"] < count["gx"] - 1
+    in_row = ((row == 0) & last_row) | ((row == nx - 1) & first_row)
+    sub = lax.rem(lane, group)
+    in_col = ((sub == 1) & (index["gy"] > 0)) | ((sub == 2) & (index["gy"] < count["gy"] - 1))
     third.wait()
+    extra.wait()
     merge(yl3, yu3)
-    half = 0.5 * DT
+    merge(el3, eu3)
+
+    def aligned(merged, f):
+        return pltpu.roll(merged[f // per], ny - group * nz * (f % per), 1) if f % per else merged[f // per]
+
+    def column_ghosts():
+        low, high = sub == 1, sub == 2
+
+        def part(f):
+            got, own = aligned(yl3, f), aligned(yp3, f)
+            above = pltpu.roll(jnp.where(high, own, got), ny - 1, 1)
+            below = pltpu.roll(jnp.where(low, own, got), 1, 1)
+            return half * (above - below), got
+
+        p0, _ = part(0)
+        p1, got = part(1)
+        diag = aligned(el3, 1)
+        pi = half * (up(0, got, diag) - down(0, got, diag)) * aligned(yl1, 5)
+        mx, my = aligned(yl2, 1), aligned(yl2, 2)
+        rho = 1.0 + aligned(yl2, 0)
+        inv = 1.0 / rho
+        zero = jnp.zeros_like(pi)
+        yr[0] = jnp.where(in_col, p0 + (p1 * mx - pi * my) * inv, zero)
+        yr[1] = jnp.where(in_col, pi, zero)
+
+    column_ghosts()
+    for e, inside in ((0, index["gz"] > 0), (nz + 1, index["gz"] < count["gz"] - 1)):
+        def plane_ghosts(e=e):
+            line, lone = lam[1, e + 1], xl[1, e]
+            pi = half * (up(0, line, lone) - down(0, line, lone)) * ge[e + 1]
+            p0 = half * (lam[0, e + 2] - lam[0, e])
+            p1 = half * (lam[1, e + 2] - lam[1, e])
+            rho = 1.0 + se1[0, e + 1]
+            zm[0, e] = p0 + (p1 * se1[1, e + 1] - pi * se1[3, e + 1]) / rho
+            zm[1, e] = pi
+
+        def plane_zeros(e=e):
+            zm[0, e] = jnp.zeros((nx, ny), jnp.float32)
+            zm[1, e] = jnp.zeros((nx, ny), jnp.float32)
+
+        pl.when(inside)(plane_ghosts)
+        pl.when(jnp.logical_not(inside))(plane_zeros)
 
     def adjoint_two(z, carry):
         u = [se1[c, z + 2] for c in range(5)]
         rho, inv, vels, internal = prim(u)
         gamma = ge[z + 2]
-        l0, l1 = lam[0, z + 1], lam[1, z + 1]
-        x0, x1 = xl[0, z], xl[1, z]
+        l0, l1 = lam[0, z + 2], lam[1, z + 2]
+        x0, x1 = xl[0, z + 1], xl[1, z + 1]
         y0, y1 = side(yl3, 0, z), side(yl3, 1, z)
-        ups0 = [up(0, l0, x0), up(1, l0, y0), lam[0, z + 2]]
-        dns0 = [down(0, l0, x0), down(1, l0, y0), lam[0, z]]
-        ups1 = [up(0, l1, x1), up(1, l1, y1), lam[1, z + 2]]
-        dns1 = [down(0, l1, x1), down(1, l1, y1), lam[1, z]]
+        ups0 = [up(0, l0, x0), up(1, l0, y0), lam[0, z + 3]]
+        dns0 = [down(0, l0, x0), down(1, l0, y0), lam[0, z + 1]]
+        ups1 = [up(0, l1, x1), up(1, l1, y1), lam[1, z + 3]]
+        dns1 = [down(0, l1, x1), down(1, l1, y1), lam[1, z + 1]]
         p0 = [half * (ups0[a] - dns0[a]) for a in range(3)]
         p1 = [half * (ups1[a] - dns1[a]) for a in range(3)]
-        ghost = half * (up(0, x1, l1) - down(0, x1, l1))
+        line = [up(0, x1, l1), down(0, x1, l1)]
+        ghost = half * (line[0] - line[1])
         sigma = kap[z] * p1[0]
         sigma_h = kah[z] * ghost
         around = ups1[0] + dns1[0] + ups1[1] + dns1[1] + ups1[2] + dns1[2]
@@ -387,7 +448,6 @@
         eps = pi * gamma * rho
         cots = [p1[a] * u[1] - eps * vels[a] for a in range(3)]
         cots[0] = cots[0] + 0.5 * (down(0, sigma, sigma_h) - up(0, sigma, sigma_h))
-        weight = 0.5 * DT * SIGNAL
         zm[0, z + 1] = p0[2] + cots[2] * inv
         zm[1, z + 1] = pi * gamma
         ze[0, z] = (
@@ -395,28 +455,40 @@
             + p1[0] * vels[0] + p1[1] * vels[1] + p1[2] * vels[2] + cots[0] * inv
         )
         ze[1, z] = pi * gamma
-        v0, g0 = ve0[0, z], vh0[z]
-        xe[z] = ze[0, z] + pi * gamma * jnp.where(row == 0, down(0, v0, g0), up(0, v0, g0))
         ze[2, z] = p0[1] + cots[1] * inv
         gam2[z] = pi * rho * internal
+
+        diag = side(el3, 1, z)
+        across = [up(1, x1, diag), down(1, x1, diag), xl[1, z + 2], xl[1, z]]
+        around = line[0] + line[1] + across[0] + across[1] + across[2] + across[3]
+        p0x = half * (up(0, x0, l0) - down(0, x0, l0))
+        py, pz = half * (across[0] - across[1]), half * (across[2] - across[3])
+        mx = xs1[1, z]
+        inv = 1.0 / (1.0 + xs1[0, z])
+        pg = ghost * xg[z]
+        v0, outer = ve0[0, z], xk[z]
+        beside = jnp.where(row == 0, pltpu.roll(v0, 1, 0), pltpu.roll(v0, nx - 1, 0))
+        cot = ghost * mx - pg * mx + 0.5 * (down(0, outer, sigma) - up(0, outer, sigma))
+        got = (
+            x1 * (1.0 - 6.0 * weight) + weight * around + p0x
+            + (ghost * mx + py * xt1[0, z] + pz * xt1[1, z] + cot) * inv + pg * beside
+        )
+        xa[z] = jnp.where(in_row, got, jnp.zeros_like(got))
         return carry
 
     loop(nz, adjoint_two, 0)
 
-    fourth.start(("gx", "gz"))
-    pack(yp4, [lambda z: ze[2, z], lambda z: ze[1, z]])
-    fourth.start(("gy",))
-    fourth.wait()
-    merge(yl4, yu4)
+    def ghost_side(k, z):
+        return pltpu.roll(yr[k], lax.rem(2 * ny - group * z - 2, ny), 1)
 
     def adjoint_one(z, acc):
         vels = [ve0[a, z] for a in range(3)]
         mx, en, my = ze[0, z], ze[1, z], ze[2, z]
-        xa = xm[z]
-        none = jnp.zeros_like(xa)
-        ya, ye = side(yl4, 0, z), side(yl4, 1, z)
+        rows = xa[z]
+        none = jnp.zeros_like(rows)
+        ya, ye = ghost_side(0, z), ghost_side(1, z)
         pi = (
-            up(0, mx, xa) - down(0, mx, xa) + up(1, my, ya) - down(1, my, ya) + zm[0, z + 2] - zm[0, z]
+            up(0, mx, rows) - down(0, mx, rows) + up(1, my, ya) - down(1, my, ya) + zm[0, z + 2] - zm[0, z]
             + vels[0] * (up(0, en, none) - down(0, en, none))
             + vels[1] * (up(1, en, ye) - down(1, en, ye))
             + vels[2] * (zm[1, z + 2] - zm[1, z])
@@ -466,7 +538,7 @@
 
     per = ny // (4 * nz)
     packs = []
-    for fields in (7, 3, 2, 2):
+    for fields in (7, 3, 2):
         packs += [vm(-(-fields // per), nx, ny)] * 3
     vmem = pl.BlockSpec(memory_space=pltpu.VMEM)
     smem = pl.BlockSpec(memory_space=pltpu.SMEM)
@@ -479,12 +551,12 @@
         scratch_shapes=[
             vm(5, nz + 4, nx, ny), vm(5, nz + 4, nx, ny), vm(nz + 4, nx, ny), vm(2, nz + 4, nx, ny, dtype=jnp.int32),
             vm(5, nz, nx, ny), vm(nz, nx, ny), vm(2, nz, nx, ny, dtype=jnp.int32),
-            vm(2, nz, nx, ny), vm(2, nz, nx, ny), vm(2, nz, nx, ny), vm(nz, nx, ny), vm(nz, nx, ny), vm(nz, nx, ny),
+            vm(2, nz, nx, ny), vm(2, nz, nx, ny), vm(2, nz, nx, ny), vm(2, nz, nx, ny), vm(nz, nx, ny), vm(nz, nx, ny),
             vm(1, count, dtype=jnp.int32), vm(1, count), vm(nz, nx, ny), vm(3, nz, nx, ny),
-            vm(2, nz, nx, ny), vm(nz, nx, ny),
+            vm(2, nz + 2, nx, ny), vm(nz, nx, ny), vm(nz, nx, ny),
             vm(3, nz, nx, ny), vm(5, nz + 2, nx, ny), vm(5, nz + 2, nx, ny), vm(2, nz + 2, nx, ny),
-            vm(nz, nx, ny), vm(nz, nx, ny), vm(nz, nx, ny), vm(2, nz + 2, nx, ny),
-            *packs,
+            vm(nz, nx, ny), vm(nz, nx, ny), vm(nz, nx, ny), vm(nz, nx, ny), vm(2, nz + 4, nx, ny), vm(2, nx, ny),
+            *packs, vm(-(-2 // per), nx, ny), vm(-(-2 // per), nx, ny),
             vm(nz * nx, ny), vm(nz * nx, ny), vm(nz * nx, ny), vm(nz * nx, count), vm(ny, count), vm(nz, nx, ny),
             vm(2, ny), vm(total, 2, ny),
             pltpu.SemaphoreType.DMA((5,)), pltpu.SemaphoreType.DMA((48,)), pltpu.SemaphoreType.DMA((48,)),

time: 30.7 us -> 28.4 us (0.925)
  Pallas kernels: 30 us -> 27.6 us
    pallas_call x1, Pallas kernels: 29.3 us -> 27 us  [local(): pl.pallas_call(functools.partial(kernel, sizes), out_shape=jax.ShapeDtype...]
where the time goes in v2:
time: 28.4 us; the launch traced here: 28.2 us
  Pallas kernels  27.6 us (97%)
  between operations  0.64 us (2%)
    pallas_call x1, Pallas kernels, local(): pl.pallas_call(functools.partial(kernel, sizes), out_shape=jax.ShapeDtype...  27 us
    pallas_call x1, Pallas kernels, local(): pl.pallas_call(store, out_shape=(jax.ShapeDtypeStruct((nz, nx, ny), f32),...  0.64 us

profile of v2, /device:TPU:0, one launch (start us, length us, event | category | flops | bytes accessed | tf_op | source)
XLA Modules:
  0.0 28.2 jit_solution(6908976858553716891)
XLA Ops:
  0.6 27.0 %adjoint.1.result = f32[17,8,128]{2,1,0:T(8,128)S(1)} custom-call(f32[5,16,8,128]{3,2,1,0:T(8,128)} %st.1, f32[16,8,128]{2,1,0:T(8,128)} %ga.1, s32[2,16,8,128]{3,2,1,0:T(8,128)} %sw.1, s32[1,256]{1,0:T(1,128)} %bitcast.3, f32[1,256]{1,0:T(1,128)} %bitcast.4), custom_call_target="tpu_custom_call" | custom-call | tf_op jit(solution)/shard_map/adjoint/pallas_call | solution.py:546
  27.6 0.6 %store.1 = (f32[16,8,128]{2,1,0:T(8,128)}, f32[1,1]{1,0:T(1,128)}) custom-call(f32[17,8,128]{2,1,0:T(8,128)S(1)} %adjoint.1.result), custom_call_target="tpu_custom_call" | custom-call | tf_op jit(solution)/shard_map/store/pallas_call | solution.py:568

commit v3 on v2

--- a/solution.py
+++ b/solution.py
@@ -1,4 +1,5 @@
 import functools
+import itertools
 import math
 
 import jax
@@ -16,6 +17,17 @@
 EPS = 1e-12
 AXES = ("gx", "gy", "gz")
 HI = lax.Precision.HIGHEST
+
+
+def lines_suffice(sizes):
+    every = list(itertools.product(*map(range, sizes)))
+    moves = [(s * (a == 0), s * (a == 1), s * (a == 2)) for a in range(3) for s in (1, -1)]
+    diagonal = [(i, j, k) for i in (1, -1) for j in (-1, 0, 1) for k in (-1, 0, 1) if (j == 0) != (k == 0)]
+    known = {d: {e for e in every if sum(a != b for a, b in zip(d, e)) <= 1} for d in every}
+    for near in (moves, moves, moves + diagonal):
+        sources = {d: [tuple(map(sum, zip(d, m))) for m in near] for d in every}
+        known = {d: known[d].union(*(known[n] for n in sources[d] if n in known)) for d in every}
+    return all(len(k) == len(every) for k in known.values())
 
 
 def kernel(
@@ -55,9 +67,15 @@
     def flat(where):
         return (where["gx"] * sizes[1] + where["gy"]) * sizes[2] + where["gz"]
 
+    def away(k):
+        parts = (k // (sizes[1] * sizes[2]), k // sizes[2] % sizes[1], k % sizes[2])
+        return sum(min(p, n - p) for p, n in zip(parts, sizes))
+
+    order = sorted(range(1, total), key=away, reverse=True)
+
     def each_peer(body):
         if total <= 64:
-            for k in range(1, total):
+            for k in order:
                 body(k)
         else:
             def step(k, carry):
@@ -65,9 +83,17 @@
                 return carry
             lax.fori_loop(1, total, step, 0)
 
-    each_peer(lambda k: pl.semaphore_signal(
-        barrier, inc=1, device_id=spot_of(k), device_id_type=pl.DeviceIdType.MESH
-    ))
+    def enter(where):
+        pl.semaphore_signal(barrier, inc=1, device_id=where, device_id_type=pl.DeviceIdType.MESH)
+
+    if lines_suffice(sizes):
+        greeted = sum(sizes) - 3
+        for a in AXES:
+            for k in sorted(range(1, count[a]), key=lambda k: min(k, count[a] - k)):
+                enter({a: lax.rem(index[a] + k, count[a])})
+    else:
+        greeted = total - 1
+        each_peer(lambda k: enter(spot_of(k)))
 
     def loop(size, body, start):
         unroll = next(u for u in (4, 3, 2, 1) if size % u == 0)
@@ -198,22 +224,25 @@
         + planes_of(lam, 2, 2) + y_copies(yp3, yl3, yu3) + edge_copies()
     )
     exchanges = (first, later, second, extra, third)
+    loads[0].wait()
+    for z in range(nz):
+        ve0[0, z] = se0[1, z + 2] / (1.0 + se0[0, z + 2])
+    loads[1].wait()
+    loads[2].wait()
+    pl.semaphore_wait(barrier, greeted)
+    first.start(("gx", "gz"))
+    pack(yp1, [lambda z, f=f: se0[f, z + 2] for f in range(5)] + [lambda z: ge[z + 2], lambda z: we[0, z + 2]])
+    first.start(("gy",))
     for exchange in exchanges:
         exchange.clear()
-    for copy in loads:
-        copy.wait()
-    for z in range(nz):
-        ve0[0, z] = se0[1, z + 2] / (1.0 + se0[0, z + 2])
-    pack(yp1, [lambda z, f=f: se0[f, z + 2] for f in range(5)] + [lambda z: ge[z + 2], lambda z: we[0, z + 2]])
+    loads[3].wait()
+    loads[4].wait()
 
     cells_row = pr[...] // ny
     cells_col = lax.rem(pr[...], ny)
     probes = pr.shape[1]
     hot_a[...] = (lax.broadcasted_iota(jnp.int32, (nz * nx, probes), 0) == cells_row).astype(jnp.float32)
     hot_b[...] = (lax.broadcasted_iota(jnp.int32, (ny, probes), 0) == cells_col).astype(jnp.float32)
-
-    pl.semaphore_wait(barrier, total - 1)
-    first.start()
 
     last_dims = (((1,), (1,)), ((), ()))
     cnt[...] = lax.dot_general(hot_a[...], hot_b[...], last_dims, precision=HI, preferred_element_type=jnp.float32)
@@ -272,6 +301,7 @@
 
     loop(nz + 2, z_pass, 0)
     first.wait(("gy",))
+    later.start()
     merge(yl1, yu1)
 
     def step_one(z, carry):
@@ -293,7 +323,6 @@
 
     loop(nz, step_one, 0)
     first.wait(("gx",))
-    later.start()
 
     def step_one_x(z, carry):
         u = [se0[c, z + 2] for c in range(5)]

time: 28.4 us -> 27.3 us (0.961)
  Pallas kernels: 27.6 us -> 26.6 us
    pallas_call x1, Pallas kernels: 27 us -> 25.9 us  [local(): pl.pallas_call(functools.partial(kernel, sizes), out_shape=jax.ShapeDtype...]
where the time goes in v3:
time: 27.3 us; the launch traced here: 27.2 us
  Pallas kernels  26.6 us (97%)
  between operations  0.64 us (2%)
    pallas_call x1, Pallas kernels, local(): pl.pallas_call(functools.partial(kernel, sizes), out_shape=jax.ShapeDtype...  25.9 us
    pallas_call x1, Pallas kernels, local(): pl.pallas_call(store, out_shape=(jax.ShapeDtypeStruct((nz, nx, ny), f32),...  0.64 us

profile of v3, /device:TPU:0, one launch (start us, length us, event | category | flops | bytes accessed | tf_op | source)
XLA Modules:
  0.0 27.2 jit_solution(12540082321522264166)
XLA Ops:
  0.6 25.9 %adjoint.1.result = f32[17,8,128]{2,1,0:T(8,128)S(1)} custom-call(f32[5,16,8,128]{3,2,1,0:T(8,128)} %st.1, f32[16,8,128]{2,1,0:T(8,128)} %ga.1, s32[2,16,8,128]{3,2,1,0:T(8,128)} %sw.1, s32[1,256]{1,0:T(1,128)} %bitcast.3, f32[1,256]{1,0:T(1,128)} %bitcast.4), custom_call_target="tpu_custom_call" | custom-call | tf_op jit(solution)/shard_map/adjoint/pallas_call | solution.py:575
  26.5 0.6 %store.1 = (f32[16,8,128]{2,1,0:T(8,128)}, f32[1,1]{1,0:T(1,128)}) custom-call(f32[17,8,128]{2,1,0:T(8,128)S(1)} %adjoint.1.result), custom_call_target="tpu_custom_call" | custom-call | tf_op jit(solution)/shard_map/store/pallas_call | solution.py:597

commit v4 on v3

--- a/solution.py
+++ b/solution.py
@@ -32,7 +32,7 @@
 
 def kernel(
     sizes, st, ga, sw, pr_in, ob_in, result,
-    se0, se1, ge, we, xs0, xg, xw, xs1, xt1, xq, q1, xv0, vh0, pr, ob, en0, ve0, xl, xk, xa, ze, az, bz, zm, kap, kah, sig, gam2,
+    se0, se1, ge, we, xs0, xg, xw, xs1, xt1, xq, q1, xv0, vh0, pr, ob, en0, ve0, xl, xk, cof, ycof, zcof, az, bz, zm, kap, kah, sig,
     lam, yr,
     yp1, yl1, yu1, yp2, yl2, yu2, yp3, yl3, yu3, el3, eu3, cnt, sob, vel, hot_a, hot_b, grad,
     mine, ar, local_sem, send_sem, recv_sem, all_send, all_recv,
@@ -41,7 +41,6 @@
     count = dict(zip(AXES, sizes))
     index = {a: lax.axis_index(a) for a in AXES}
     total = math.prod(sizes)
-    me = (index["gx"] * sizes[1] + index["gy"]) * sizes[2] + index["gz"]
     group = 4
     per = ny // (group * nz)
 
@@ -63,9 +62,6 @@
         else:
             parts = (k // (sizes[1] * sizes[2]), lax.rem(k // sizes[2], sizes[1]), lax.rem(k, sizes[2]))
         return {a: lax.rem(index[a] + parts[i], count[a]) for i, a in enumerate(AXES)}
-
-    def flat(where):
-        return (where["gx"] * sizes[1] + where["gy"]) * sizes[2] + where["gz"]
 
     def away(k):
         parts = (k // (sizes[1] * sizes[2]), k // sizes[2] % sizes[1], k % sizes[2])
@@ -315,7 +311,7 @@
         for c in range(5):
             change = dy[c] + az[c, z + 2] - bz[c, z] + 3.0 * SIGNAL * u[c]
             se1[c, z + 2] = u[c] - DT * change
-        en0[z] = energy
+        en0[z] = 0.5 * DT * energy
         for a in range(1, 3):
             ve0[a, z] = vels[a]
         q1[1, z] = p
@@ -357,8 +353,8 @@
         v, v_h = q1[0, z], jnp.where(edge, xs1[1, z] / (1.0 + xs1[0, z]), xq[0, z])
         squeeze = jnp.minimum(0.5 * (up(0, v, v_h) - down(0, v, v_h)), 0.0)
         squeeze_h = jnp.minimum(0.5 * (up(0, v_h, v) - down(0, v_h, v)), 0.0)
-        kap[z] = 2.0 * s * squeeze
-        kah[z] = 2.0 * sh * squeeze_h
+        kap[z] = DT * s * squeeze
+        kah[z] = DT * sh * squeeze_h
 
         def along(r, mx, speed, t):
             f = [0.5 * mx, 0.5 * (mx * speed + t)]
@@ -409,13 +405,44 @@
     in_row = ((row == 0) & last_row) | ((row == nx - 1) & first_row)
     sub = lax.rem(lane, group)
     in_col = ((sub == 1) & (index["gy"] > 0)) | ((sub == 2) & (index["gy"] < count["gy"] - 1))
+    z_sides = ((0, index["gz"] > 0), (nz + 1, index["gz"] < count["gz"] - 1))
+    extra.wait()
+
+    def aligned(merged, f):
+        return pltpu.roll(merged[f // per], ny - group * nz * (f % per), 1) if f % per else merged[f // per]
+
+    inv = half / (1.0 + aligned(yl2, 0))
+    gamma = aligned(yl1, 5)
+    ycof[0] = aligned(yl2, 1) * inv
+    ycof[1] = aligned(yl2, 2) * inv * gamma
+    ycof[2] = half * gamma
+    for k, (e, _) in enumerate(z_sides):
+        inv = half / (1.0 + se1[0, e + 1])
+        zcof[k, 0] = se1[1, e + 1] * inv
+        zcof[k, 1] = se1[3, e + 1] * inv * ge[e + 1]
+        zcof[k, 2] = half * ge[e + 1]
+
+    def coefficients(z, carry):
+        rho, inv, vels, internal = prim([se1[c, z + 2] for c in range(5)])
+        gamma = ge[z + 2]
+        vx, vy, vz = [half * v for v in vels]
+        v0 = ve0[0, z]
+        beside = jnp.where(row == 0, pltpu.roll(v0, 1, 0), pltpu.roll(v0, nx - 1, 0))
+        inv_h = 1.0 / (1.0 + xs1[0, z])
+        gamma_h = xg[z]
+        rows = [
+            (2.0 - gamma) * vx, vx, vy, vz, gamma * vy, gamma * vz, half * gamma, half * rho * internal, 0.5 * inv,
+            half * ((2.0 - gamma_h) * xs1[1, z] * inv_h + gamma_h * beside), half * xt1[0, z] * inv_h,
+            half * xt1[1, z] * inv_h, 0.5 * inv_h,
+        ]
+        for k, value in enumerate(rows):
+            cof[z, k] = value
+        return carry
+
+    loop(nz, coefficients, 0)
     third.wait()
-    extra.wait()
     merge(yl3, yu3)
     merge(el3, eu3)
-
-    def aligned(merged, f):
-        return pltpu.roll(merged[f // per], ny - group * nz * (f % per), 1) if f % per else merged[f // per]
 
     def column_ghosts():
         low, high = sub == 1, sub == 2
@@ -424,29 +451,24 @@
             got, own = aligned(yl3, f), aligned(yp3, f)
             above = pltpu.roll(jnp.where(high, own, got), ny - 1, 1)
             below = pltpu.roll(jnp.where(low, own, got), 1, 1)
-            return half * (above - below), got
-
-        p0, _ = part(0)
-        p1, got = part(1)
+            return above - below, got
+
+        d0, _ = part(0)
+        d1, got = part(1)
         diag = aligned(el3, 1)
-        pi = half * (up(0, got, diag) - down(0, got, diag)) * aligned(yl1, 5)
-        mx, my = aligned(yl2, 1), aligned(yl2, 2)
-        rho = 1.0 + aligned(yl2, 0)
-        inv = 1.0 / rho
-        zero = jnp.zeros_like(pi)
-        yr[0] = jnp.where(in_col, p0 + (p1 * mx - pi * my) * inv, zero)
-        yr[1] = jnp.where(in_col, pi, zero)
+        dx = up(0, got, diag) - down(0, got, diag)
+        zero = jnp.zeros_like(dx)
+        yr[0] = jnp.where(in_col, half * d0 + d1 * ycof[0] - dx * ycof[1], zero)
+        yr[1] = jnp.where(in_col, dx * ycof[2], zero)
 
     column_ghosts()
-    for e, inside in ((0, index["gz"] > 0), (nz + 1, index["gz"] < count["gz"] - 1)):
-        def plane_ghosts(e=e):
+    for k, (e, inside) in enumerate(z_sides):
+        def plane_ghosts(e=e, k=k):
             line, lone = lam[1, e + 1], xl[1, e]
-            pi = half * (up(0, line, lone) - down(0, line, lone)) * ge[e + 1]
-            p0 = half * (lam[0, e + 2] - lam[0, e])
-            p1 = half * (lam[1, e + 2] - lam[1, e])
-            rho = 1.0 + se1[0, e + 1]
-            zm[0, e] = p0 + (p1 * se1[1, e + 1] - pi * se1[3, e + 1]) / rho
-            zm[1, e] = pi
+            dx = up(0, line, lone) - down(0, line, lone)
+            d0, d1 = lam[0, e + 2] - lam[0, e], lam[1, e + 2] - lam[1, e]
+            zm[0, e] = half * d0 + d1 * zcof[k, 0] - dx * zcof[k, 1]
+            zm[1, e] = dx * zcof[k, 2]
 
         def plane_zeros(e=e):
             zm[0, e] = jnp.zeros((nx, ny), jnp.float32)
@@ -455,99 +477,81 @@
         pl.when(inside)(plane_ghosts)
         pl.when(jnp.logical_not(inside))(plane_zeros)
 
-    def adjoint_two(z, carry):
-        u = [se1[c, z + 2] for c in range(5)]
-        rho, inv, vels, internal = prim(u)
-        gamma = ge[z + 2]
+    def ghost_side(k, z):
+        return pltpu.roll(yr[k], lax.rem(2 * ny - group * z - 2, ny), 1)
+
+    def adjoint(z, carry):
+        ca, cx, cy, cz, gy, gz, gg, gr, ci, ka, ky, kz, ki = [cof[z, k] for k in range(13)]
         l0, l1 = lam[0, z + 2], lam[1, z + 2]
         x0, x1 = xl[0, z + 1], xl[1, z + 1]
         y0, y1 = side(yl3, 0, z), side(yl3, 1, z)
-        ups0 = [up(0, l0, x0), up(1, l0, y0), lam[0, z + 3]]
-        dns0 = [down(0, l0, x0), down(1, l0, y0), lam[0, z + 1]]
-        ups1 = [up(0, l1, x1), up(1, l1, y1), lam[1, z + 3]]
-        dns1 = [down(0, l1, x1), down(1, l1, y1), lam[1, z + 1]]
-        p0 = [half * (ups0[a] - dns0[a]) for a in range(3)]
-        p1 = [half * (ups1[a] - dns1[a]) for a in range(3)]
-        line = [up(0, x1, l1), down(0, x1, l1)]
-        ghost = half * (line[0] - line[1])
-        sigma = kap[z] * p1[0]
-        sigma_h = kah[z] * ghost
-        around = ups1[0] + dns1[0] + ups1[1] + dns1[1] + ups1[2] + dns1[2]
-        pi = p1[0]
-        eps = pi * gamma * rho
-        cots = [p1[a] * u[1] - eps * vels[a] for a in range(3)]
-        cots[0] = cots[0] + 0.5 * (down(0, sigma, sigma_h) - up(0, sigma, sigma_h))
-        zm[0, z + 1] = p0[2] + cots[2] * inv
-        zm[1, z + 1] = pi * gamma
-        ze[0, z] = (
-            l1 * (1.0 - 6.0 * weight) + weight * around + p0[0]
-            + p1[0] * vels[0] + p1[1] * vels[1] + p1[2] * vels[2] + cots[0] * inv
+        diag = side(el3, 1, z)
+        xu, xd = up(0, l1, x1), down(0, l1, x1)
+        yu, yd = up(1, l1, y1), down(1, l1, y1)
+        zu, zd = lam[1, z + 3], lam[1, z + 1]
+        gu, gd = up(0, x1, l1), down(0, x1, l1)
+        eu, ed = up(1, x1, diag), down(1, x1, diag)
+        fu, fd = xl[1, z + 2], xl[1, z]
+        dx, dy, dz, dg = xu - xd, yu - yd, zu - zd, gu - gd
+        sigma, sigma_h, outer = kap[z] * dx, kah[z] * dg, xk[z]
+        en = gg * dx
+        zm[0, z + 1] = half * (lam[0, z + 3] - lam[0, z + 1]) + cx * dz - gz * dx
+        zm[1, z + 1] = en
+        my = half * (up(1, l0, y0) - down(1, l0, y0)) + cx * dy - gy * dx
+        mx = (
+            (1.0 - 6.0 * weight) * l1 + weight * ((xu + xd) + (yu + yd) + (zu + zd))
+            + half * (up(0, l0, x0) - down(0, l0, x0)) + ca * dx + cy * dy + cz * dz
+            + ci * (down(0, sigma, sigma_h) - up(0, sigma, sigma_h))
         )
-        ze[1, z] = pi * gamma
-        ze[2, z] = p0[1] + cots[1] * inv
-        gam2[z] = pi * rho * internal
-
-        diag = side(el3, 1, z)
-        across = [up(1, x1, diag), down(1, x1, diag), xl[1, z + 2], xl[1, z]]
-        around = line[0] + line[1] + across[0] + across[1] + across[2] + across[3]
-        p0x = half * (up(0, x0, l0) - down(0, x0, l0))
-        py, pz = half * (across[0] - across[1]), half * (across[2] - across[3])
-        mx = xs1[1, z]
-        inv = 1.0 / (1.0 + xs1[0, z])
-        pg = ghost * xg[z]
-        v0, outer = ve0[0, z], xk[z]
-        beside = jnp.where(row == 0, pltpu.roll(v0, 1, 0), pltpu.roll(v0, nx - 1, 0))
-        cot = ghost * mx - pg * mx + 0.5 * (down(0, outer, sigma) - up(0, outer, sigma))
-        got = (
-            x1 * (1.0 - 6.0 * weight) + weight * around + p0x
-            + (ghost * mx + py * xt1[0, z] + pz * xt1[1, z] + cot) * inv + pg * beside
+        rows = (
+            (1.0 - 6.0 * weight) * x1 + weight * ((gu + gd) + (eu + ed) + (fu + fd))
+            + half * (up(0, x0, l0) - down(0, x0, l0)) + ka * dg + ky * (eu - ed) + kz * (fu - fd)
+            + ki * (down(0, outer, sigma) - up(0, outer, sigma))
         )
-        xa[z] = jnp.where(in_row, got, jnp.zeros_like(got))
-        return carry
-
-    loop(nz, adjoint_two, 0)
-
-    def ghost_side(k, z):
-        return pltpu.roll(yr[k], lax.rem(2 * ny - group * z - 2, ny), 1)
-
-    def adjoint_one(z, acc):
-        vels = [ve0[a, z] for a in range(3)]
-        mx, en, my = ze[0, z], ze[1, z], ze[2, z]
-        rows = xa[z]
-        none = jnp.zeros_like(rows)
+        zero = jnp.zeros_like(rows)
+        rows = jnp.where(in_row, rows, zero)
         ya, ye = ghost_side(0, z), ghost_side(1, z)
         pi = (
-            up(0, mx, rows) - down(0, mx, rows) + up(1, my, ya) - down(1, my, ya) + zm[0, z + 2] - zm[0, z]
-            + vels[0] * (up(0, en, none) - down(0, en, none))
-            + vels[1] * (up(1, en, ye) - down(1, en, ye))
-            + vels[2] * (zm[1, z + 2] - zm[1, z])
+            up(0, mx, rows) - down(0, mx, rows) + up(1, my, ya) - down(1, my, ya)
+            + ve0[0, z] * (up(0, en, zero) - down(0, en, zero)) + ve0[1, z] * (up(1, en, ye) - down(1, en, ye))
         )
-        g = gam2[z] + half * pi * en0[z]
+        grad[z] = gr * dx + en0[z] * pi
+        return carry
+
+    loop(nz, adjoint, 0)
+
+    def along_z(z, acc):
+        g = grad[z] + en0[z] * (zm[0, z + 2] - zm[0, z] + ve0[2, z] * (zm[1, z + 2] - zm[1, z]))
         grad[z] = g
         return acc + g * g
 
-    square = loop(nz, adjoint_one, jnp.zeros((nx, ny), jnp.float32))
-    mine[pl.ds(0, 1), :] = jnp.sum(square, axis=0, keepdims=True)
-    mine[pl.ds(1, 1), :] = miss
-    def all_copy(k, slot_at):
+    square = loop(nz, along_z, jnp.zeros((nx, ny), jnp.float32))
+    def folded(x):
+        return x + pltpu.roll(x, ny // 2, 1)
+
+    low_half = lane[0:1] < ny // 2
+    mine[...] = jnp.where(low_half, folded(jnp.sum(square, axis=0, keepdims=True)), folded(miss))
+
+    def all_copy(k):
         return pltpu.make_async_remote_copy(
-            src_ref=mine, dst_ref=ar.at[slot_at], send_sem=all_send.at[k], recv_sem=all_recv.at[slot_at],
+            src_ref=mine, dst_ref=ar.at[k], send_sem=all_send.at[k], recv_sem=all_recv.at[k],
             device_id=spot_of(k), device_id_type=pl.DeviceIdType.MESH,
         )
 
-    each_peer(lambda k: all_copy(k, me).start())
-    ar[me] = mine[...]
+    each_peer(lambda k: all_copy(k).start())
+    ar[0] = mine[...]
     for exchange in exchanges:
         exchange.finish()
-    each_peer(lambda k: all_copy(k, flat(spot_of(k))).wait_recv())
+    each_peer(lambda k: all_copy(k).wait_send())
+    each_peer(lambda k: all_copy(k).wait_recv())
     sums = jnp.sum(ar[...], axis=0)
+    zero = jnp.zeros_like(sums)
     cells = total * nz * nx * ny
-    mean = jnp.sum(sums[0:1, :], axis=1, keepdims=True) / cells
-    misfit = jnp.sum(sums[1:2, :], axis=1, keepdims=True) / (total * probes)
+    mean = jnp.sum(jnp.where(low_half, sums, zero), axis=1, keepdims=True) / cells
+    misfit = jnp.sum(jnp.where(low_half, zero, sums), axis=1, keepdims=True) / (total * probes)
     scale = 1.0 / jnp.sqrt(mean + EPS)
     result[pl.ds(0, nz)] = grad[...] * jnp.broadcast_to(scale, (nx, ny))
     result[nz] = jnp.broadcast_to(misfit, (nx, ny))
-    each_peer(lambda k: all_copy(k, me).wait_send())
 
 
 def store(result, direction, misfit):
@@ -582,12 +586,12 @@
             vm(5, nz, nx, ny), vm(nz, nx, ny), vm(2, nz, nx, ny, dtype=jnp.int32),
             vm(2, nz, nx, ny), vm(2, nz, nx, ny), vm(2, nz, nx, ny), vm(2, nz, nx, ny), vm(nz, nx, ny), vm(nz, nx, ny),
             vm(1, count, dtype=jnp.int32), vm(1, count), vm(nz, nx, ny), vm(3, nz, nx, ny),
-            vm(2, nz + 2, nx, ny), vm(nz, nx, ny), vm(nz, nx, ny),
-            vm(3, nz, nx, ny), vm(5, nz + 2, nx, ny), vm(5, nz + 2, nx, ny), vm(2, nz + 2, nx, ny),
-            vm(nz, nx, ny), vm(nz, nx, ny), vm(nz, nx, ny), vm(nz, nx, ny), vm(2, nz + 4, nx, ny), vm(2, nx, ny),
+            vm(2, nz + 2, nx, ny), vm(nz, nx, ny), vm(nz, 13, nx, ny), vm(3, nx, ny), vm(2, 3, nx, ny),
+            vm(5, nz + 2, nx, ny), vm(5, nz + 2, nx, ny), vm(2, nz + 2, nx, ny),
+            vm(nz, nx, ny), vm(nz, nx, ny), vm(nz, nx, ny), vm(2, nz + 4, nx, ny), vm(2, nx, ny),
             *packs, vm(-(-2 // per), nx, ny), vm(-(-2 // per), nx, ny),
             vm(nz * nx, ny), vm(nz * nx, ny), vm(nz * nx, ny), vm(nz * nx, count), vm(ny, count), vm(nz, nx, ny),
-            vm(2, ny), vm(total, 2, ny),
+            vm(1, ny), vm(total, 1, ny),
             pltpu.SemaphoreType.DMA((5,)), pltpu.SemaphoreType.DMA((48,)), pltpu.SemaphoreType.DMA((48,)),
             pltpu.SemaphoreType.DMA((total,)), pltpu.SemaphoreType.DMA((total,)),
         ],

time: 27.3 us -> 27 us (0.989)
  Pallas kernels: 26.6 us -> 26.2 us
    pallas_call x1, Pallas kernels: 25.9 us -> 25.5 us  [local(): pl.pallas_call(functools.partial(kernel, sizes), out_shape=jax.ShapeDtype...]
where the time goes in v4:
time: 27 us; the launch traced here: 26.8 us
  Pallas kernels  26.2 us (97%)
  between operations  0.64 us (2%)
    pallas_call x1, Pallas kernels, local(): pl.pallas_call(functools.partial(kernel, sizes), out_shape=jax.ShapeDtype...  25.5 us
    pallas_call x1, Pallas kernels, local(): pl.pallas_call(store, out_shape=(jax.ShapeDtypeStruct((nz, nx, ny), f32),...  0.64 us

profile of v4, /device:TPU:0, one launch (start us, length us, event | category | flops | bytes accessed | tf_op | source)
XLA Modules:
  0.0 26.8 jit_solution(13944186453776196890)
XLA Ops:
  0.6 25.5 %adjoint.1.result = f32[17,8,128]{2,1,0:T(8,128)S(1)} custom-call(f32[5,16,8,128]{3,2,1,0:T(8,128)} %st.1, f32[16,8,128]{2,1,0:T(8,128)} %ga.1, s32[2,16,8,128]{3,2,1,0:T(8,128)} %sw.1, s32[1,256]{1,0:T(1,128)} %bitcast.3, f32[1,256]{1,0:T(1,128)} %bitcast.4), custom_call_target="tpu_custom_call" | custom-call | tf_op jit(solution)/shard_map/adjoint/pallas_call | solution.py:579
  26.2 0.6 %store.1 = (f32[16,8,128]{2,1,0:T(8,128)}, f32[1,1]{1,0:T(1,128)}) custom-call(f32[17,8,128]{2,1,0:T(8,128)S(1)} %adjoint.1.result), custom_call_target="tpu_custom_call" | custom-call | tf_op jit(solution)/shard_map/store/pallas_call | solution.py:601

commit v5 on v4

--- a/solution.py
+++ b/solution.py
@@ -91,8 +91,8 @@
         greeted = total - 1
         each_peer(lambda k: enter(spot_of(k)))
 
-    def loop(size, body, start):
-        unroll = next(u for u in (4, 3, 2, 1) if size % u == 0)
+    def loop(size, body, start, most=4):
+        unroll = next(u for u in range(most, 0, -1) if size % u == 0)
 
         def several(i, carry):
             for j in range(unroll):
@@ -336,7 +336,7 @@
         q1[1, z] = press(new, ge[z + 2], rho, internal)
         return carry
 
-    loop(nz, step_one_x, 0)
+    loop(nz, step_one_x, 0, 8)
     second.start(("gx", "gz"))
     pack(yp2, [lambda z, f=f: se1[f, z + 2] for f in range(3)])
     second.start(("gy",))
@@ -388,7 +388,7 @@
         sig[z] = s * squeeze * DT * (pltpu.roll(w, nx - 1, 0) - pltpu.roll(w, 1, 0))
         return carry
 
-    loop(nz, step_two, 0)
+    loop(nz, step_two, 0, 16)
 
     third.start(("gx", "gz"))
     pack(yp3, [lambda z, f=f: lam[f, z + 2] for f in range(2)])
@@ -518,14 +518,14 @@
         grad[z] = gr * dx + en0[z] * pi
         return carry
 
-    loop(nz, adjoint, 0)
+    loop(nz, adjoint, 0, 8)
 
     def along_z(z, acc):
         g = grad[z] + en0[z] * (zm[0, z + 2] - zm[0, z] + ve0[2, z] * (zm[1, z + 2] - zm[1, z]))
         grad[z] = g
         return acc + g * g
 
-    square = loop(nz, along_z, jnp.zeros((nx, ny), jnp.float32))
+    square = loop(nz, along_z, jnp.zeros((nx, ny), jnp.float32), 4)
     def folded(x):
         return x + pltpu.roll(x, ny // 2, 1)
 

time: 27 us -> 26.2 us (0.970)
  Pallas kernels: 26.2 us -> 25.4 us
    pallas_call x1, Pallas kernels: 25.5 us -> 24.7 us  [local(): pl.pallas_call(functools.partial(kernel, sizes), out_shape=jax.ShapeDtype...]
where the time goes in v5:
time: 26.2 us; the launch traced here: 26 us
  Pallas kernels  25.4 us (97%)
  between operations  0.64 us (2%)
    pallas_call x1, Pallas kernels, local(): pl.pallas_call(functools.partial(kernel, sizes), out_shape=jax.ShapeDtype...  24.7 us
    pallas_call x1, Pallas kernels, local(): pl.pallas_call(store, out_shape=(jax.ShapeDtypeStruct((nz, nx, ny), f32),...  0.64 us

profile of v5, /device:TPU:0, one launch (start us, length us, event | category | flops | bytes accessed | tf_op | source)
XLA Modules:
  0.0 26.0 jit_solution(8410902590202765713)
XLA Ops:
  0.6 24.7 %adjoint.1.result = f32[17,8,128]{2,1,0:T(8,128)S(1)} custom-call(f32[5,16,8,128]{3,2,1,0:T(8,128)} %st.1, f32[16,8,128]{2,1,0:T(8,128)} %ga.1, s32[2,16,8,128]{3,2,1,0:T(8,128)} %sw.1, s32[1,256]{1,0:T(1,128)} %bitcast.3, f32[1,256]{1,0:T(1,128)} %bitcast.4), custom_call_target="tpu_custom_call" | custom-call | tf_op jit(solution)/shard_map/adjoint/pallas_call | solution.py:579
  25.4 0.6 %store.1 = (f32[16,8,128]{2,1,0:T(8,128)}, f32[1,1]{1,0:T(1,128)}) custom-call(f32[17,8,128]{2,1,0:T(8,128)S(1)} %adjoint.1.result), custom_call_target="tpu_custom_call" | custom-call | tf_op jit(solution)/shard_map/store/pallas_call | solution.py:601

commit v6 on v5

--- a/solution.py
+++ b/solution.py
@@ -32,7 +32,7 @@
 
 def kernel(
     sizes, st, ga, sw, pr_in, ob_in, result,
-    se0, se1, ge, we, xs0, xg, xw, xs1, xt1, xq, q1, xv0, vh0, pr, ob, en0, ve0, xl, xk, cof, ycof, zcof, az, bz, zm, kap, kah, sig,
+    se0, se1, ge, we, xs0, xg, xw, xs1, xt1, xq, q1, xv0, pr, ob, en0, ve0, xl, xm, xk, cof, ycof, zcof, az, bz, zm, kap, kah, sig,
     lam, yr,
     yp1, yl1, yu1, yp2, yl2, yu2, yp3, yl3, yu3, el3, eu3, cnt, sob, vel, hot_a, hot_b, grad,
     mine, ar, local_sem, send_sem, recv_sem, all_send, all_recv,
@@ -105,13 +105,17 @@
     row = lax.broadcasted_iota(jnp.int32, (nx, ny), 0)
 
     def up(axis, own, ghost):
-        at = (row if axis == 0 else lane) == 0
-        return pltpu.roll(jnp.where(at, ghost, own), own.shape[axis] - 1, axis)
+        if axis == 0:
+            return jnp.where(row == nx - 1, ghost, pltpu.roll(own, nx - 1, 0))
+        return pltpu.roll(jnp.where(lane == 0, ghost, own), ny - 1, 1)
 
     def down(axis, own, ghost):
-        size = own.shape[axis]
-        at = (row if axis == 0 else lane) == size - 1
-        return pltpu.roll(jnp.where(at, ghost, own), 1, axis)
+        if axis == 0:
+            return jnp.where(row == 0, ghost, pltpu.roll(own, 1, 0))
+        return pltpu.roll(jnp.where(lane == ny - 1, ghost, own), 1, 1)
+
+    sign = jnp.where(row == 0, -1.0, 1.0)
+    sign_y = jnp.where(lane == 0, -1.0, jnp.where(lane == ny - 1, 1.0, 0.0))
 
     slot = [0]
 
@@ -157,12 +161,14 @@
                 if copy is not None:
                     pl.when(sends)(copy.wait_send)
 
-    def rows_of(src, dst, first, depth, skip=0, start=0):
-        hi, lo = pl.ds(nx - depth - skip, depth), pl.ds(skip, depth)
+    top, bottom = pl.ds(nx - 1, 1), pl.ds(0, 1)
+
+    def rows_of(src, dst, first, skip=0, start=0):
+        hi, lo = pl.ds(nx - 1 - skip, 1), pl.ds(skip, 1)
         lead = (slice(None),) * (len(dst.shape) - 3)
         return [
-            ("gx", {"gx": 1}, src.at[lead + (pl.ds(first, nz), hi)], dst.at[lead + (pl.ds(start, nz), hi)]),
-            ("gx", {"gx": -1}, src.at[lead + (pl.ds(first, nz), lo)], dst.at[lead + (pl.ds(start, nz), lo)]),
+            ("gx", {"gx": 1}, src.at[lead + (pl.ds(first, nz), hi)], dst.at[lead + (pl.ds(start, nz), bottom)]),
+            ("gx", {"gx": -1}, src.at[lead + (pl.ds(first, nz), lo)], dst.at[lead + (pl.ds(start, nz), top)]),
         ]
 
     def planes_of(src, first, depth, pick=slice(None), lead=True):
@@ -196,27 +202,27 @@
 
     def edge_copies():
         copies = []
-        for sx, line in ((1, pl.ds(nx - 1, 1)), (-1, pl.ds(0, 1))):
+        for sx, line, spot in ((1, top, bottom), (-1, bottom, top)):
             for sy, dst in ((1, el3), (-1, eu3)):
-                copies.append(("edge", {"gx": sx, "gy": sy}, yp3.at[:, line], dst.at[:, line]))
+                copies.append(("edge", {"gx": sx, "gy": sy}, yp3.at[:, line], dst.at[:, spot]))
             for sz, src, dst in ((1, nz + 1, 0), (-1, 2, nz + 1)):
-                copies.append(("edge", {"gx": sx, "gz": sz}, lam.at[1, src, line], xl.at[1, dst, line]))
+                copies.append(("edge", {"gx": sx, "gz": sz}, lam.at[1, src, line], xl.at[1, dst, spot]))
         return copies
 
     first = Exchange(
-        rows_of(se0, xs0, 2, 1) + rows_of(ve0.at[0], xv0, 0, 1, 1)
-        + rows_of(ge, xg, 2, 1) + rows_of(we.at[0], xw.at[0], 2, 1)
+        rows_of(se0, xs0, 2) + rows_of(ve0.at[0], xv0, 0, 1)
+        + rows_of(ge, xg, 2) + rows_of(we.at[0], xw.at[0], 2)
         + planes_of(se0, 2, 2) + planes_of(ge, 2, 2, lead=False) + planes_of(we, 2, 2)
         + y_copies(yp1, yl1, yu1)
     )
-    later = Exchange(rows_of(we.at[1], xw.at[1], 2, 1))
+    later = Exchange(rows_of(we.at[1], xw.at[1], 2))
     second = Exchange(
-        rows_of(se1.at[pl.ds(0, 2)], xs1, 2, 1) + rows_of(q1.at[0], xq.at[0], 0, 1, 1)
-        + rows_of(q1.at[1], xq.at[1], 0, 1) + planes_of(se1, 2, 1) + y_copies(yp2, yl2, yu2)
+        rows_of(se1.at[pl.ds(0, 2)], xs1, 2) + rows_of(q1.at[0], xq.at[0], 0, 1)
+        + rows_of(q1.at[1], xq.at[1], 0) + planes_of(se1, 2, 1) + y_copies(yp2, yl2, yu2)
     )
-    extra = Exchange(rows_of(se1.at[pl.ds(2, 2)], xt1, 2, 1))
+    extra = Exchange(rows_of(se1.at[pl.ds(2, 2)], xt1, 2))
     third = Exchange(
-        rows_of(lam, xl, 2, 2, 0, 1) + rows_of(sig, xk, 0, 1, 1)
+        rows_of(lam, xl, 2, 0, 1) + rows_of(lam, xm, 2, 1) + rows_of(sig, xk, 0, 1)
         + planes_of(lam, 2, 2) + y_copies(yp3, yl3, yu3) + edge_copies()
     )
     exchanges = (first, later, second, extra, third)
@@ -231,6 +237,7 @@
     first.start(("gy",))
     for exchange in exchanges:
         exchange.clear()
+    xl[:, :, pl.ds(1, nx - 2)] = jnp.zeros((2, nz + 2, nx - 2, ny), jnp.float32)
     loads[3].wait()
     loads[4].wait()
 
@@ -265,20 +272,19 @@
         b_side = [0.5 * f[c] + 0.5 * SIGNAL * u[c] for c in range(5)]
         return a_side, b_side
 
-    edge = (row == 0) | (row == nx - 1)
-
     def paired(a, axis, u, pv, uh, gh, sh, s, far=None):
         rho, _, vels, _, p = pv
         rho_h, _, vels_h, e_h = prim(uh)
         p_h = press(uh, gh, rho_h, e_h)
         v, v_h = vels[a], vels_h[a]
-        if far is not None:
-            v_h = jnp.where(edge, v_h, far)
         slope = 0.5 * (up(axis, v, v_h) - down(axis, v, v_h))
-        slope_h = 0.5 * (up(axis, v_h, v) - down(axis, v_h, v))
+        if far is None:
+            slope_h = 0.5 * (up(axis, v_h, v) - down(axis, v_h, v))
+        else:
+            slope_h = 0.5 * sign * (far - v)
         ao, bo = flux(a, u, v, p, rho, s, slope)
         ah, bh = flux(a, uh, v_h, p_h, rho_h, sh, slope_h)
-        return [up(axis, ao[c], ah[c]) - down(axis, bo[c], bh[c]) for c in range(5)], v_h
+        return [up(axis, ao[c], ah[c]) - down(axis, bo[c], bh[c]) for c in range(5)]
 
     first.wait(("gz",))
 
@@ -307,7 +313,7 @@
         p = press(u, ge[z + 2], rho, internal)
         s = we[0, z + 2].astype(jnp.float32)
         pv = (rho, inv, vels, internal, p)
-        dy = paired(1, 1, u, pv, [side(yl1, c, z) for c in range(5)], side(yl1, 5, z), side(yl1, 6, z), s)[0]
+        dy = paired(1, 1, u, pv, [side(yl1, c, z) for c in range(5)], side(yl1, 5, z), side(yl1, 6, z), s)
         for c in range(5):
             change = dy[c] + az[c, z + 2] - bz[c, z] + 3.0 * SIGNAL * u[c]
             se1[c, z + 2] = u[c] - DT * change
@@ -325,7 +331,7 @@
         rho = 1.0 + u[0]
         s = we[0, z + 2].astype(jnp.float32)
         pv = (rho, None, [ve0[0, z]], None, q1[1, z])
-        dx, vh0[z] = paired(
+        dx = paired(
             0, 0, u, pv, [xs0[c, z] for c in range(5)], xg[z], xw[0, z].astype(jnp.float32), s, xv0[z]
         )
         new = [se1[c, z + 2] - DT * dx[c] for c in range(5)]
@@ -350,9 +356,9 @@
         u = [se1[c, z + 2] for c in range(4)]
         s = we[1, z + 2].astype(jnp.float32) * QUAD * (1.0 + u[0])
         sh = xw[1, z].astype(jnp.float32) * QUAD * (1.0 + xs1[0, z])
-        v, v_h = q1[0, z], jnp.where(edge, xs1[1, z] / (1.0 + xs1[0, z]), xq[0, z])
+        v, v_h = q1[0, z], xs1[1, z] / (1.0 + xs1[0, z])
         squeeze = jnp.minimum(0.5 * (up(0, v, v_h) - down(0, v, v_h)), 0.0)
-        squeeze_h = jnp.minimum(0.5 * (up(0, v_h, v) - down(0, v_h, v)), 0.0)
+        squeeze_h = jnp.minimum(0.5 * sign * (xq[0, z] - v), 0.0)
         kap[z] = DT * s * squeeze
         kah[z] = DT * sh * squeeze_h
 
@@ -402,19 +408,22 @@
     half = 0.5 * DT
     weight = 0.5 * DT * SIGNAL
     first_row, last_row = index["gx"] > 0, index["gx"] < count["gx"] - 1
-    in_row = ((row == 0) & last_row) | ((row == nx - 1) & first_row)
+    in_row = ((row == 0) & first_row) | ((row == nx - 1) & last_row)
     sub = lax.rem(lane, group)
-    in_col = ((sub == 1) & (index["gy"] > 0)) | ((sub == 2) & (index["gy"] < count["gy"] - 1))
+    in_col = ((sub == 2) & (index["gy"] > 0)) | ((sub == 1) & (index["gy"] < count["gy"] - 1))
     z_sides = ((0, index["gz"] > 0), (nz + 1, index["gz"] < count["gz"] - 1))
     extra.wait()
 
     def aligned(merged, f):
         return pltpu.roll(merged[f // per], ny - group * nz * (f % per), 1) if f % per else merged[f // per]
 
-    inv = half / (1.0 + aligned(yl2, 0))
-    gamma = aligned(yl1, 5)
-    ycof[0] = aligned(yl2, 1) * inv
-    ycof[1] = aligned(yl2, 2) * inv * gamma
+    def turned(x):
+        return jnp.where(sub == 1, pltpu.roll(x, ny - 1, 1), pltpu.roll(x, 1, 1))
+
+    inv = half / (1.0 + turned(aligned(yl2, 0)))
+    gamma = turned(aligned(yl1, 5))
+    ycof[0] = turned(aligned(yl2, 1)) * inv
+    ycof[1] = turned(aligned(yl2, 2)) * inv * gamma
     ycof[2] = half * gamma
     for k, (e, _) in enumerate(z_sides):
         inv = half / (1.0 + se1[0, e + 1])
@@ -422,18 +431,28 @@
         zcof[k, 1] = se1[3, e + 1] * inv * ge[e + 1]
         zcof[k, 2] = half * ge[e + 1]
 
+    def shifts(axis, x):
+        at, size = (row, nx) if axis == 0 else (lane, ny)
+        zero = jnp.zeros_like(x)
+        above = jnp.where(at == size - 1, zero, pltpu.roll(x, size - 1, axis))
+        below = jnp.where(at == 0, zero, pltpu.roll(x, 1, axis))
+        return above, below
+
     def coefficients(z, carry):
         rho, inv, vels, internal = prim([se1[c, z + 2] for c in range(5)])
         gamma = ge[z + 2]
         vx, vy, vz = [half * v for v in vels]
-        v0 = ve0[0, z]
-        beside = jnp.where(row == 0, pltpu.roll(v0, 1, 0), pltpu.roll(v0, nx - 1, 0))
         inv_h = 1.0 / (1.0 + xs1[0, z])
         gamma_h = xg[z]
+        l0, l1 = lam[0, z + 2], lam[1, z + 2]
+        (xu, xd), (yu, yd) = shifts(0, l1), shifts(1, l1)
+        (xu0, xd0), (yu0, yd0) = shifts(0, l0), shifts(1, l0)
+        ka = half * sign * ((2.0 - gamma_h) * xs1[1, z] * inv_h + gamma_h * ve0[0, z])
         rows = [
             (2.0 - gamma) * vx, vx, vy, vz, gamma * vy, gamma * vz, half * gamma, half * rho * internal, 0.5 * inv,
-            half * ((2.0 - gamma_h) * xs1[1, z] * inv_h + gamma_h * beside), half * xt1[0, z] * inv_h,
-            half * xt1[1, z] * inv_h, 0.5 * inv_h,
+            weight + ka, half * xt1[0, z] * inv_h, half * xt1[1, z] * inv_h, 0.5 * sign * inv_h, xu - xd,
+            (1.0 - 6.0 * weight) * l1 + weight * ((xu + xd) + (yu + yd)) + half * (xu0 - xd0) + vy * (yu - yd),
+            half * (yu0 - yd0) + vx * (yu - yd), weight * l1 - half * sign * l0 - ka * l1,
         ]
         for k, value in enumerate(rows):
             cof[z, k] = value
@@ -441,27 +460,24 @@
 
     loop(nz, coefficients, 0)
     third.wait()
-    merge(yl3, yu3)
-    merge(el3, eu3)
-
-    def column_ghosts():
-        low, high = sub == 1, sub == 2
-
-        def part(f):
-            got, own = aligned(yl3, f), aligned(yp3, f)
-            above = pltpu.roll(jnp.where(high, own, got), ny - 1, 1)
-            below = pltpu.roll(jnp.where(low, own, got), 1, 1)
-            return above - below, got
-
-        d0, _ = part(0)
-        d1, got = part(1)
-        diag = aligned(el3, 1)
-        dx = up(0, got, diag) - down(0, got, diag)
-        zero = jnp.zeros_like(dx)
-        yr[0] = jnp.where(in_col, half * d0 + d1 * ycof[0] - dx * ycof[1], zero)
-        yr[1] = jnp.where(in_col, dx * ycof[2], zero)
-
-    column_ghosts()
+
+    def packed_ghosts(low, high, reach):
+        return [
+            jnp.where(sub < 2, pltpu.roll(high[k], ny - reach, 1), pltpu.roll(low[k], reach, 1))
+            for k in range(low.shape[0])
+        ]
+
+    near, next_ = packed_ghosts(yl3, yu3, 1), packed_ghosts(yl3, yu3, 2)
+    diagonal = packed_ghosts(el3, eu3, 1)
+    for k in range(len(near)):
+        yl3[k], el3[k] = near[k], diagonal[k]
+    turn = jnp.where(sub == 1, 1.0, -1.0)
+    got, diag = aligned(near, 1), aligned(diagonal, 1)
+    d0, d1 = [turn * (aligned(next_, f) - aligned(yp3, f)) for f in range(2)]
+    dx = up(0, got, diag) - down(0, got, diag)
+    zero = jnp.zeros_like(dx)
+    yr[0] = jnp.where(in_col, half * d0 + d1 * ycof[0] - dx * ycof[1], zero)
+    yr[1] = jnp.where(in_col, dx * ycof[2], zero)
     for k, (e, inside) in enumerate(z_sides):
         def plane_ghosts(e=e, k=k):
             line, lone = lam[1, e + 1], xl[1, e]
@@ -480,40 +496,41 @@
     def ghost_side(k, z):
         return pltpu.roll(yr[k], lax.rem(2 * ny - group * z - 2, ny), 1)
 
+    def across(x, ghost):
+        above = jnp.where(lane == ny - 1, ghost, pltpu.roll(x, ny - 1, 1))
+        return above, jnp.where(lane == 0, ghost, pltpu.roll(x, 1, 1))
+
+    at_side = (lane == 0) | (lane == ny - 1)
+
     def adjoint(z, carry):
-        ca, cx, cy, cz, gy, gz, gg, gr, ci, ka, ky, kz, ki = [cof[z, k] for k in range(13)]
-        l0, l1 = lam[0, z + 2], lam[1, z + 2]
-        x0, x1 = xl[0, z + 1], xl[1, z + 1]
-        y0, y1 = side(yl3, 0, z), side(yl3, 1, z)
-        diag = side(el3, 1, z)
-        xu, xd = up(0, l1, x1), down(0, l1, x1)
-        yu, yd = up(1, l1, y1), down(1, l1, y1)
-        zu, zd = lam[1, z + 3], lam[1, z + 1]
-        gu, gd = up(0, x1, l1), down(0, x1, l1)
-        eu, ed = up(1, x1, diag), down(1, x1, diag)
-        fu, fd = xl[1, z + 2], xl[1, z]
-        dx, dy, dz, dg = xu - xd, yu - yd, zu - zd, gu - gd
-        sigma, sigma_h, outer = kap[z] * dx, kah[z] * dg, xk[z]
+        ca, cx, cy, cz, gy, gz, gg, gr, ci, ka, ky, kz, ki, dx, mx, my, rows = [cof[z, k] for k in range(17)]
+        l1, x0, x1, x2 = lam[1, z + 2], xl[0, z + 1], xl[1, z + 1], xm[1, z]
+        zero = jnp.zeros_like(dx)
+        y1 = jnp.where(at_side, side(yl3, 1, z), zero)
+        y1_turn = sign_y * y1
+        eu, ed = across(x1, side(el3, 1, z))
+        zu, zd, fu, fd = lam[1, z + 3], lam[1, z + 1], xl[1, z + 2], xl[1, z]
+        dx = dx + sign * x1
+        dz = zu - zd
+        sigma, sigma_h = kap[z] * dx, kah[z] * (sign * (x2 - l1))
         en = gg * dx
         zm[0, z + 1] = half * (lam[0, z + 3] - lam[0, z + 1]) + cx * dz - gz * dx
         zm[1, z + 1] = en
-        my = half * (up(1, l0, y0) - down(1, l0, y0)) + cx * dy - gy * dx
+        my = my + half * sign_y * side(yl3, 0, z) + cx * y1_turn - gy * dx
         mx = (
-            (1.0 - 6.0 * weight) * l1 + weight * ((xu + xd) + (yu + yd) + (zu + zd))
-            + half * (up(0, l0, x0) - down(0, l0, x0)) + ca * dx + cy * dy + cz * dz
+            mx + weight * ((x1 + y1) + (zu + zd)) + half * sign * x0 + ca * dx + cy * y1_turn + cz * dz
             + ci * (down(0, sigma, sigma_h) - up(0, sigma, sigma_h))
         )
         rows = (
-            (1.0 - 6.0 * weight) * x1 + weight * ((gu + gd) + (eu + ed) + (fu + fd))
-            + half * (up(0, x0, l0) - down(0, x0, l0)) + ka * dg + ky * (eu - ed) + kz * (fu - fd)
-            + ki * (down(0, outer, sigma) - up(0, outer, sigma))
+            rows + (1.0 - 6.0 * weight) * x1 + weight * ((eu + ed) + (fu + fd)) + half * sign * xm[0, z] + ka * x2
+            + ky * (eu - ed) + kz * (fu - fd) + ki * (sigma - xk[z])
         )
-        zero = jnp.zeros_like(rows)
         rows = jnp.where(in_row, rows, zero)
-        ya, ye = ghost_side(0, z), ghost_side(1, z)
+        yu, yd = across(my, ghost_side(0, z))
+        eu, ed = across(en, ghost_side(1, z))
         pi = (
-            up(0, mx, rows) - down(0, mx, rows) + up(1, my, ya) - down(1, my, ya)
-            + ve0[0, z] * (up(0, en, zero) - down(0, en, zero)) + ve0[1, z] * (up(1, en, ye) - down(1, en, ye))
+            up(0, mx, rows) - down(0, mx, rows) + (yu - yd)
+            + ve0[0, z] * (up(0, en, zero) - down(0, en, zero)) + ve0[1, z] * (eu - ed)
         )
         grad[z] = gr * dx + en0[z] * pi
         return carry
@@ -584,9 +601,9 @@
         scratch_shapes=[
             vm(5, nz + 4, nx, ny), vm(5, nz + 4, nx, ny), vm(nz + 4, nx, ny), vm(2, nz + 4, nx, ny, dtype=jnp.int32),
             vm(5, nz, nx, ny), vm(nz, nx, ny), vm(2, nz, nx, ny, dtype=jnp.int32),
-            vm(2, nz, nx, ny), vm(2, nz, nx, ny), vm(2, nz, nx, ny), vm(2, nz, nx, ny), vm(nz, nx, ny), vm(nz, nx, ny),
+            vm(2, nz, nx, ny), vm(2, nz, nx, ny), vm(2, nz, nx, ny), vm(2, nz, nx, ny), vm(nz, nx, ny),
             vm(1, count, dtype=jnp.int32), vm(1, count), vm(nz, nx, ny), vm(3, nz, nx, ny),
-            vm(2, nz + 2, nx, ny), vm(nz, nx, ny), vm(nz, 13, nx, ny), vm(3, nx, ny), vm(2, 3, nx, ny),
+            vm(2, nz + 2, nx, ny), vm(2, nz, nx, ny), vm(nz, nx, ny), vm(nz, 17, nx, ny), vm(3, nx, ny), vm(2, 3, nx, ny),
             vm(5, nz + 2, nx, ny), vm(5, nz + 2, nx, ny), vm(2, nz + 2, nx, ny),
             vm(nz, nx, ny), vm(nz, nx, ny), vm(nz, nx, ny), vm(2, nz + 4, nx, ny), vm(2, nx, ny),
             *packs, vm(-(-2 // per), nx, ny), vm(-(-2 // per), nx, ny),

time: 26.2 us -> 26 us (level)
  no operation moved by 1% of the time
where the time goes in v6:
time: 26 us; the launch traced here: 25.8 us
  Pallas kernels  25.2 us (97%)
  between operations  0.64 us (2%)
    pallas_call x1, Pallas kernels, local(): pl.pallas_call(functools.partial(kernel, sizes), out_shape=jax.ShapeDtype...  24.5 us
    pallas_call x1, Pallas kernels, local(): pl.pallas_call(store, out_shape=(jax.ShapeDtypeStruct((nz, nx, ny), f32),...  0.64 us

profile of v6, /device:TPU:0, one launch (start us, length us, event | category | flops | bytes accessed | tf_op | source)
XLA Modules:
  0.0 25.8 jit_solution(5319788871281489155)
XLA Ops:
  0.6 24.5 %adjoint.1.result = f32[17,8,128]{2,1,0:T(8,128)S(1)} custom-call(f32[5,16,8,128]{3,2,1,0:T(8,128)} %st.1, f32[16,8,128]{2,1,0:T(8,128)} %ga.1, s32[2,16,8,128]{3,2,1,0:T(8,128)} %sw.1, s32[1,256]{1,0:T(1,128)} %bitcast.3, f32[1,256]{1,0:T(1,128)} %bitcast.4), custom_call_target="tpu_custom_call" | custom-call | tf_op jit(solution)/shard_map/adjoint/pallas_call | solution.py:596
  25.2 0.6 %store.1 = (f32[16,8,128]{2,1,0:T(8,128)}, f32[1,1]{1,0:T(1,128)}) custom-call(f32[17,8,128]{2,1,0:T(8,128)S(1)} %adjoint.1.result), custom_call_target="tpu_custom_call" | custom-call | tf_op jit(solution)/shard_map/store/pallas_call | solution.py:618

commit v7 on v6

--- a/solution.py
+++ b/solution.py
@@ -32,7 +32,7 @@
 
 def kernel(
     sizes, st, ga, sw, pr_in, ob_in, result,
-    se0, se1, ge, we, xs0, xg, xw, xs1, xt1, xq, q1, xv0, pr, ob, en0, ve0, xl, xm, xk, cof, ycof, zcof, az, bz, zm, kap, kah, sig,
+    se0, se1, ge, we, xs0, xg, xw, xs1, xt1, xq, q1, xv0, pr, ob, en0, ve0, xl, xm, xk, part, cof, ycof, zcof, az, bz, zm, kap, kah, sig,
     lam, yr,
     yp1, yl1, yu1, yp2, yl2, yu2, yp3, yl3, yu3, el3, eu3, cnt, sob, vel, hot_a, hot_b, grad,
     mine, ar, local_sem, send_sem, recv_sem, all_send, all_recv,
@@ -146,12 +146,12 @@
                 else:
                     pl.when(jnp.logical_not(receives))(zero)
 
-        def start(self, axes=AXES + ("edge",)):
+        def start(self, axes=AXES + ("edge", "gx2", "gz2")):
             for axis, _, copy, sends, _ in self.copies:
                 if copy is not None and axis in axes:
                     pl.when(sends)(copy.start)
 
-        def wait(self, axes=AXES + ("edge",)):
+        def wait(self, axes=AXES + ("edge", "gx2", "gz2")):
             for axis, _, copy, _, receives in self.copies:
                 if copy is not None and axis in axes:
                     pl.when(receives)(copy.wait_recv)
@@ -163,20 +163,20 @@
 
     top, bottom = pl.ds(nx - 1, 1), pl.ds(0, 1)
 
-    def rows_of(src, dst, first, skip=0, start=0):
+    def rows_of(src, dst, first, skip=0, start=0, name="gx"):
         hi, lo = pl.ds(nx - 1 - skip, 1), pl.ds(skip, 1)
         lead = (slice(None),) * (len(dst.shape) - 3)
         return [
-            ("gx", {"gx": 1}, src.at[lead + (pl.ds(first, nz), hi)], dst.at[lead + (pl.ds(start, nz), bottom)]),
-            ("gx", {"gx": -1}, src.at[lead + (pl.ds(first, nz), lo)], dst.at[lead + (pl.ds(start, nz), top)]),
+            (name, {"gx": 1}, src.at[lead + (pl.ds(first, nz), hi)], dst.at[lead + (pl.ds(start, nz), bottom)]),
+            (name, {"gx": -1}, src.at[lead + (pl.ds(first, nz), lo)], dst.at[lead + (pl.ds(start, nz), top)]),
         ]
 
-    def planes_of(src, first, depth, pick=slice(None), lead=True):
+    def planes_of(src, first, depth, pick=slice(None), lead=True, name="gz"):
         def at(start):
             return src.at[pick, pl.ds(start, depth)] if lead else src.at[pl.ds(start, depth)]
         return [
-            ("gz", {"gz": 1}, at(first + nz - depth), at(first - depth)),
-            ("gz", {"gz": -1}, at(first), at(first + nz)),
+            (name, {"gz": 1}, at(first + nz - depth), at(first - depth)),
+            (name, {"gz": -1}, at(first), at(first + nz)),
         ]
 
     def pack(dst, fields):
@@ -210,14 +210,15 @@
         return copies
 
     first = Exchange(
-        rows_of(se0, xs0, 2) + rows_of(ve0.at[0], xv0, 0, 1)
-        + rows_of(ge, xg, 2) + rows_of(we.at[0], xw.at[0], 2)
-        + planes_of(se0, 2, 2) + planes_of(ge, 2, 2, lead=False) + planes_of(we, 2, 2)
+        rows_of(se0, xs0, 2) + planes_of(se0, 2, 2)
+        + rows_of(ge, xg, 2, name="gx2") + rows_of(we.at[0], xw.at[0], 2, name="gx2")
+        + rows_of(ve0.at[0], xv0, 0, 1, name="gx2")
+        + planes_of(ge, 2, 2, lead=False, name="gz2") + planes_of(we, 2, 2, name="gz2")
         + y_copies(yp1, yl1, yu1)
     )
     later = Exchange(rows_of(we.at[1], xw.at[1], 2))
     second = Exchange(
-        rows_of(se1.at[pl.ds(0, 2)], xs1, 2) + rows_of(q1.at[0], xq.at[0], 0, 1)
+        rows_of(se1.at[0], xs1.at[0], 2) + rows_of(q1.at[0], xs1.at[1], 0) + rows_of(q1.at[0], xq.at[0], 0, 1)
         + rows_of(q1.at[1], xq.at[1], 0) + planes_of(se1, 2, 1) + y_copies(yp2, yl2, yu2)
     )
     extra = Exchange(rows_of(se1.at[pl.ds(2, 2)], xt1, 2))
@@ -227,12 +228,13 @@
     )
     exchanges = (first, later, second, extra, third)
     loads[0].wait()
+    pl.semaphore_wait(barrier, greeted)
+    first.start(("gx", "gz"))
     for z in range(nz):
         ve0[0, z] = se0[1, z + 2] / (1.0 + se0[0, z + 2])
     loads[1].wait()
     loads[2].wait()
-    pl.semaphore_wait(barrier, greeted)
-    first.start(("gx", "gz"))
+    first.start(("gx2", "gz2"))
     pack(yp1, [lambda z, f=f: se0[f, z + 2] for f in range(5)] + [lambda z: ge[z + 2], lambda z: we[0, z + 2]])
     first.start(("gy",))
     for exchange in exchanges:
@@ -286,7 +288,7 @@
         ah, bh = flux(a, uh, v_h, p_h, rho_h, sh, slope_h)
         return [up(axis, ao[c], ah[c]) - down(axis, bo[c], bh[c]) for c in range(5)]
 
-    first.wait(("gz",))
+    first.wait(("gz", "gz2"))
 
     def z_pass(e, carry):
         u = [se0[c, e + 1] for c in range(5)]
@@ -303,7 +305,6 @@
 
     loop(nz + 2, z_pass, 0)
     first.wait(("gy",))
-    later.start()
     merge(yl1, yu1)
 
     def step_one(z, carry):
@@ -324,7 +325,8 @@
         return carry
 
     loop(nz, step_one, 0)
-    first.wait(("gx",))
+    first.wait(("gx", "gx2"))
+    later.start()
 
     def step_one_x(z, carry):
         u = [se0[c, z + 2] for c in range(5)]
@@ -347,43 +349,85 @@
     pack(yp2, [lambda z, f=f: se1[f, z + 2] for f in range(3)])
     second.start(("gy",))
     extra.start()
-    second.wait(("gz", "gy"))
-    merge(yl2, yu2)
-    second.wait(("gx",))
+    sub = lax.rem(lane, group)
+    turn = jnp.where(sub == 1, 1.0, -1.0)
+    at_side = (lane == 0) | (lane == ny - 1)
+    at_end = (row == 0) | (row == nx - 1)
+    lean = 0.5 * SIGNAL
+
+    def aligned(merged, f):
+        return pltpu.roll(merged[f // per], ny - group * nz * (f % per), 1) if f % per else merged[f // per]
+
+    def packed_ghosts(low, high, reach):
+        return [
+            jnp.where(sub < 2, pltpu.roll(high[k], ny - reach, 1), pltpu.roll(low[k], reach, 1))
+            for k in range(low.shape[0])
+        ]
+
+    def shifts(axis, x):
+        at, size = (row, nx) if axis == 0 else (lane, ny)
+        zero = jnp.zeros_like(x)
+        above = jnp.where(at == size - 1, zero, pltpu.roll(x, size - 1, axis))
+        below = jnp.where(at == 0, zero, pltpu.roll(x, 1, axis))
+        return above, below
+
+    def z_flux(e):
+        r, mx, mz = se1[0, e + 1], se1[1, e + 1], se1[3, e + 1]
+        flows = [0.5 * mz, 0.5 * mx * (mz / (1.0 + r))]
+        for c, flow in enumerate(flows):
+            az[c, e] = flow - lean * (r, mx)[c]
+            bz[c, e] = flow + lean * (r, mx)[c]
+
+    def own_part(z, carry):
+        r, mx, my = [se1[c, z + 2] for c in range(3)]
+        v = q1[0, z]
+        above, below = shifts(0, v)
+        xflows, yflows = [0.5 * mx, 0.5 * (mx * v + q1[1, z])], [0.5 * my, 0.5 * mx * (my / (1.0 + r))]
+        for c, u in enumerate((r, mx)):
+            change = 6.0 * lean * u
+            for axis, flows in ((0, xflows), (1, yflows)):
+                change = change + shifts(axis, flows[c] - lean * u)[0] - shifts(axis, flows[c] + lean * u)[1]
+            part[z, c] = u - DT * change
+        part[z, 2] = 0.5 * (above - below)
+        part[z, 3] = we[1, z + 2].astype(jnp.float32) * QUAD * (1.0 + r)
+        z_flux(z + 1)
+        return carry
+
+    loop(nz, own_part, 0)
     later.wait()
+    second.wait()
+    for e in (0, nz + 1):
+        z_flux(e)
+    got = packed_ghosts(yl2, yu2, 1)
+    for k in range(len(got)):
+        yl2[k] = got[k]
+    r, mx, my = [aligned(got, f) for f in range(3)]
+    yr[0] = turn * (0.5 * my) - lean * r
+    yr[1] = turn * (0.5 * mx * (my / (1.0 + r))) - lean * mx
+
+    def ghost_side(k, z):
+        return pltpu.roll(yr[k], lax.rem(2 * ny - group * z - 2, ny), 1)
 
     def step_two(z, carry):
-        u = [se1[c, z + 2] for c in range(4)]
-        s = we[1, z + 2].astype(jnp.float32) * QUAD * (1.0 + u[0])
-        sh = xw[1, z].astype(jnp.float32) * QUAD * (1.0 + xs1[0, z])
-        v, v_h = q1[0, z], xs1[1, z] / (1.0 + xs1[0, z])
-        squeeze = jnp.minimum(0.5 * (up(0, v, v_h) - down(0, v, v_h)), 0.0)
-        squeeze_h = jnp.minimum(0.5 * sign * (xq[0, z] - v), 0.0)
-        kap[z] = DT * s * squeeze
-        kah[z] = DT * sh * squeeze_h
-
-        def along(r, mx, speed, t):
-            f = [0.5 * mx, 0.5 * (mx * speed + t)]
-            d = [0.5 * SIGNAL * r, 0.5 * SIGNAL * mx]
-            return [f[0] - d[0], f[1] - d[1]], [f[0] + d[0], f[1] + d[1]]
-
-        ax, bx = along(u[0], u[1], v, q1[1, z] + s * squeeze * squeeze)
-        axh, bxh = along(xs1[0, z], xs1[1, z], v_h, xq[1, z] + sh * squeeze_h * squeeze_h)
-        dx = [up(0, ax[c], axh[c]) - down(0, bx[c], bxh[c]) for c in range(2)]
-
-        def simple(r, mx, ma):
-            f = [0.5 * ma, 0.5 * mx * (ma / (1.0 + r))]
-            d = [0.5 * SIGNAL * r, 0.5 * SIGNAL * mx]
-            return [f[0] - d[0], f[1] - d[1]], [f[0] + d[0], f[1] + d[1]]
-
-        ao, bo = simple(u[0], u[1], u[2])
-        ah, bh = simple(side(yl2, 0, z), side(yl2, 1, z), side(yl2, 2, z))
-        above = simple(se1[0, z + 3], se1[1, z + 3], se1[3, z + 3])[0]
-        below = simple(se1[0, z + 1], se1[1, z + 1], se1[3, z + 1])[1]
+        r_h, v_h, far, p_h = xs1[0, z], xs1[1, z], xq[0, z], xq[1, z]
+        rho_h = 1.0 + r_h
+        mx_h = rho_h * v_h
+        s, sh = part[z, 3], xw[1, z].astype(jnp.float32) * QUAD * rho_h
+        zero = jnp.zeros_like(r_h)
+        squeeze = jnp.minimum(part[z, 2] + jnp.where(at_end, 0.5 * sign * v_h, zero), 0.0)
+        squeeze_h = jnp.minimum(0.5 * sign * (far - q1[0, z]), 0.0)
+        slope, slope_h = s * squeeze, sh * squeeze_h
+        kap[z] = DT * slope
+        kah[z] = DT * slope_h
+        above, below = shifts(0, 0.5 * slope * squeeze)
+        ghosts = [sign * (0.5 * mx_h) - lean * r_h, sign * (0.5 * (mx_h * v_h + p_h + slope_h * squeeze_h)) - lean * mx_h]
         new = []
         for c in range(2):
-            change = dx[c] + up(1, ao[c], ah[c]) - down(1, bo[c], bh[c]) + above[c] - below[c] + 3.0 * SIGNAL * u[c]
-            new.append(u[c] - DT * change)
+            change = jnp.where(at_end, ghosts[c], zero) + jnp.where(at_side, ghost_side(c, z), zero)
+            change = change + az[c, z + 2] - bz[c, z]
+            if c == 1:
+                change = change + above - below
+            new.append(part[z, c] - DT * change)
         inv2 = 1.0 / (1.0 + new[0])
         v = new[1] * inv2
         at = pl.ds(pl.multiple_of(z * nx, nx), nx)
@@ -391,7 +435,7 @@
         w = 2.0 * (cnt[at, :] * v - sob[at, :]) * inv2
         lam[0, z + 2] = -w * v
         lam[1, z + 2] = w
-        sig[z] = s * squeeze * DT * (pltpu.roll(w, nx - 1, 0) - pltpu.roll(w, 1, 0))
+        sig[z] = DT * slope * (pltpu.roll(w, nx - 1, 0) - pltpu.roll(w, 1, 0))
         return carry
 
     loop(nz, step_two, 0, 16)
@@ -409,34 +453,23 @@
     weight = 0.5 * DT * SIGNAL
     first_row, last_row = index["gx"] > 0, index["gx"] < count["gx"] - 1
     in_row = ((row == 0) & first_row) | ((row == nx - 1) & last_row)
-    sub = lax.rem(lane, group)
     in_col = ((sub == 2) & (index["gy"] > 0)) | ((sub == 1) & (index["gy"] < count["gy"] - 1))
     z_sides = ((0, index["gz"] > 0), (nz + 1, index["gz"] < count["gz"] - 1))
     extra.wait()
 
-    def aligned(merged, f):
-        return pltpu.roll(merged[f // per], ny - group * nz * (f % per), 1) if f % per else merged[f // per]
-
     def turned(x):
         return jnp.where(sub == 1, pltpu.roll(x, ny - 1, 1), pltpu.roll(x, 1, 1))
 
-    inv = half / (1.0 + turned(aligned(yl2, 0)))
+    inv = half / (1.0 + aligned(yl2, 0))
     gamma = turned(aligned(yl1, 5))
-    ycof[0] = turned(aligned(yl2, 1)) * inv
-    ycof[1] = turned(aligned(yl2, 2)) * inv * gamma
+    ycof[0] = aligned(yl2, 1) * inv
+    ycof[1] = aligned(yl2, 2) * inv * gamma
     ycof[2] = half * gamma
     for k, (e, _) in enumerate(z_sides):
         inv = half / (1.0 + se1[0, e + 1])
         zcof[k, 0] = se1[1, e + 1] * inv
         zcof[k, 1] = se1[3, e + 1] * inv * ge[e + 1]
         zcof[k, 2] = half * ge[e + 1]
-
-    def shifts(axis, x):
-        at, size = (row, nx) if axis == 0 else (lane, ny)
-        zero = jnp.zeros_like(x)
-        above = jnp.where(at == size - 1, zero, pltpu.roll(x, size - 1, axis))
-        below = jnp.where(at == 0, zero, pltpu.roll(x, 1, axis))
-        return above, below
 
     def coefficients(z, carry):
         rho, inv, vels, internal = prim([se1[c, z + 2] for c in range(5)])
@@ -447,7 +480,7 @@
         l0, l1 = lam[0, z + 2], lam[1, z + 2]
         (xu, xd), (yu, yd) = shifts(0, l1), shifts(1, l1)
         (xu0, xd0), (yu0, yd0) = shifts(0, l0), shifts(1, l0)
-        ka = half * sign * ((2.0 - gamma_h) * xs1[1, z] * inv_h + gamma_h * ve0[0, z])
+        ka = half * sign * ((2.0 - gamma_h) * xs1[1, z] + gamma_h * ve0[0, z])
         rows = [
             (2.0 - gamma) * vx, vx, vy, vz, gamma * vy, gamma * vz, half * gamma, half * rho * internal, 0.5 * inv,
             weight + ka, half * xt1[0, z] * inv_h, half * xt1[1, z] * inv_h, 0.5 * sign * inv_h, xu - xd,
@@ -461,17 +494,10 @@
     loop(nz, coefficients, 0)
     third.wait()
 
-    def packed_ghosts(low, high, reach):
-        return [
-            jnp.where(sub < 2, pltpu.roll(high[k], ny - reach, 1), pltpu.roll(low[k], reach, 1))
-            for k in range(low.shape[0])
-        ]
-
     near, next_ = packed_ghosts(yl3, yu3, 1), packed_ghosts(yl3, yu3, 2)
     diagonal = packed_ghosts(el3, eu3, 1)
     for k in range(len(near)):
         yl3[k], el3[k] = near[k], diagonal[k]
-    turn = jnp.where(sub == 1, 1.0, -1.0)
     got, diag = aligned(near, 1), aligned(diagonal, 1)
     d0, d1 = [turn * (aligned(next_, f) - aligned(yp3, f)) for f in range(2)]
     dx = up(0, got, diag) - down(0, got, diag)
@@ -493,14 +519,9 @@
         pl.when(inside)(plane_ghosts)
         pl.when(jnp.logical_not(inside))(plane_zeros)
 
-    def ghost_side(k, z):
-        return pltpu.roll(yr[k], lax.rem(2 * ny - group * z - 2, ny), 1)
-
     def across(x, ghost):
         above = jnp.where(lane == ny - 1, ghost, pltpu.roll(x, ny - 1, 1))
         return above, jnp.where(lane == 0, ghost, pltpu.roll(x, 1, 1))
-
-    at_side = (lane == 0) | (lane == ny - 1)
 
     def adjoint(z, carry):
         ca, cx, cy, cz, gy, gz, gg, gr, ci, ka, ky, kz, ki, dx, mx, my, rows = [cof[z, k] for k in range(17)]
@@ -603,13 +624,13 @@
             vm(5, nz, nx, ny), vm(nz, nx, ny), vm(2, nz, nx, ny, dtype=jnp.int32),
             vm(2, nz, nx, ny), vm(2, nz, nx, ny), vm(2, nz, nx, ny), vm(2, nz, nx, ny), vm(nz, nx, ny),
             vm(1, count, dtype=jnp.int32), vm(1, count), vm(nz, nx, ny), vm(3, nz, nx, ny),
-            vm(2, nz + 2, nx, ny), vm(2, nz, nx, ny), vm(nz, nx, ny), vm(nz, 17, nx, ny), vm(3, nx, ny), vm(2, 3, nx, ny),
+            vm(2, nz + 2, nx, ny), vm(2, nz, nx, ny), vm(nz, nx, ny), vm(nz, 4, nx, ny), vm(nz, 17, nx, ny), vm(3, nx, ny), vm(2, 3, nx, ny),
             vm(5, nz + 2, nx, ny), vm(5, nz + 2, nx, ny), vm(2, nz + 2, nx, ny),
             vm(nz, nx, ny), vm(nz, nx, ny), vm(nz, nx, ny), vm(2, nz + 4, nx, ny), vm(2, nx, ny),
             *packs, vm(-(-2 // per), nx, ny), vm(-(-2 // per), nx, ny),
             vm(nz * nx, ny), vm(nz * nx, ny), vm(nz * nx, ny), vm(nz * nx, count), vm(ny, count), vm(nz, nx, ny),
             vm(1, ny), vm(total, 1, ny),
-            pltpu.SemaphoreType.DMA((5,)), pltpu.SemaphoreType.DMA((48,)), pltpu.SemaphoreType.DMA((48,)),
+            pltpu.SemaphoreType.DMA((5,)), pltpu.SemaphoreType.DMA((64,)), pltpu.SemaphoreType.DMA((64,)),
             pltpu.SemaphoreType.DMA((total,)), pltpu.SemaphoreType.DMA((total,)),
         ],
         compiler_params=pltpu.CompilerParams(collective_id=0, has_side_effects=True, vmem_limit_bytes=32 << 20),

time: 26 us -> 26 us (level)
  no operation moved by 1% of the time
where the time goes in v7:
time: 26 us; the launch traced here: 25.9 us
  Pallas kernels  25.2 us (97%)
  between operations  0.64 us (2%)
    pallas_call x1, Pallas kernels, local(): pl.pallas_call(functools.partial(kernel, sizes), out_shape=jax.ShapeDtype...  24.6 us
    pallas_call x1, Pallas kernels, local(): pl.pallas_call(store, out_shape=(jax.ShapeDtypeStruct((nz, nx, ny), f32),...  0.64 us

profile of v7, /device:TPU:0, one launch (start us, length us, event | category | flops | bytes accessed | tf_op | source)
XLA Modules:
  0.0 25.9 jit_solution(3706136532098707908)
XLA Ops:
  0.6 24.6 %adjoint.1.result = f32[17,8,128]{2,1,0:T(8,128)S(1)} custom-call(f32[5,16,8,128]{3,2,1,0:T(8,128)} %st.1, f32[16,8,128]{2,1,0:T(8,128)} %ga.1, s32[2,16,8,128]{3,2,1,0:T(8,128)} %sw.1, s32[1,256]{1,0:T(1,128)} %bitcast.3, f32[1,256]{1,0:T(1,128)} %bitcast.4), custom_call_target="tpu_custom_call" | custom-call | tf_op jit(solution)/shard_map/adjoint/pallas_call | solution.py:617
  25.2 0.6 %store.1 = (f32[16,8,128]{2,1,0:T(8,128)}, f32[1,1]{1,0:T(1,128)}) custom-call(f32[17,8,128]{2,1,0:T(8,128)S(1)} %adjoint.1.result), custom_call_target="tpu_custom_call" | custom-call | tf_op jit(solution)/shard_map/store/pallas_call | solution.py:639

commit v8 on v7

--- a/solution.py
+++ b/solution.py
@@ -223,7 +223,7 @@
     )
     extra = Exchange(rows_of(se1.at[pl.ds(2, 2)], xt1, 2))
     third = Exchange(
-        rows_of(lam, xl, 2, 0, 1) + rows_of(lam, xm, 2, 1) + rows_of(sig, xk, 0, 1)
+        rows_of(lam, xl, 2, 0, 1) + rows_of(lam.at[1], xm, 2, 1) + rows_of(sig, xk, 0, 1)
         + planes_of(lam, 2, 2) + y_copies(yp3, yl3, yu3) + edge_copies()
     )
     exchanges = (first, later, second, extra, third)
@@ -390,6 +390,8 @@
             part[z, c] = u - DT * change
         part[z, 2] = 0.5 * (above - below)
         part[z, 3] = we[1, z + 2].astype(jnp.float32) * QUAD * (1.0 + r)
+        inv = 0.5 / (1.0 + r)
+        part[z, 4] = jnp.where(row < nx // 2, pltpu.roll(inv, 1, 0), pltpu.roll(inv, nx - 1, 0))
         z_flux(z + 1)
         return carry
 
@@ -433,9 +435,11 @@
         at = pl.ds(pl.multiple_of(z * nx, nx), nx)
         vel[at, :] = v
         w = 2.0 * (cnt[at, :] * v - sob[at, :]) * inv2
-        lam[0, z + 2] = -w * v
+        lam0 = -w * v
+        lam[0, z + 2] = lam0
         lam[1, z + 2] = w
-        sig[z] = DT * slope * (pltpu.roll(w, nx - 1, 0) - pltpu.roll(w, 1, 0))
+        sigma = DT * slope * (pltpu.roll(w, nx - 1, 0) - pltpu.roll(w, 1, 0))
+        sig[z] = 0.5 * DT * lam0 - part[z, 4] * sigma
         return carry
 
     loop(nz, step_two, 0, 16)
@@ -525,7 +529,7 @@
 
     def adjoint(z, carry):
         ca, cx, cy, cz, gy, gz, gg, gr, ci, ka, ky, kz, ki, dx, mx, my, rows = [cof[z, k] for k in range(17)]
-        l1, x0, x1, x2 = lam[1, z + 2], xl[0, z + 1], xl[1, z + 1], xm[1, z]
+        l1, x0, x1, x2 = lam[1, z + 2], xl[0, z + 1], xl[1, z + 1], xm[z]
         zero = jnp.zeros_like(dx)
         y1 = jnp.where(at_side, side(yl3, 1, z), zero)
         y1_turn = sign_y * y1
@@ -543,8 +547,8 @@
             + ci * (down(0, sigma, sigma_h) - up(0, sigma, sigma_h))
         )
         rows = (
-            rows + (1.0 - 6.0 * weight) * x1 + weight * ((eu + ed) + (fu + fd)) + half * sign * xm[0, z] + ka * x2
-            + ky * (eu - ed) + kz * (fu - fd) + ki * (sigma - xk[z])
+            rows + (1.0 - 6.0 * weight) * x1 + weight * ((eu + ed) + (fu + fd)) + sign * xk[z] + ka * x2
+            + ky * (eu - ed) + kz * (fu - fd) + ki * sigma
         )
         rows = jnp.where(in_row, rows, zero)
         yu, yd = across(my, ghost_side(0, z))
@@ -624,7 +628,7 @@
             vm(5, nz, nx, ny), vm(nz, nx, ny), vm(2, nz, nx, ny, dtype=jnp.int32),
             vm(2, nz, nx, ny), vm(2, nz, nx, ny), vm(2, nz, nx, ny), vm(2, nz, nx, ny), vm(nz, nx, ny),
             vm(1, count, dtype=jnp.int32), vm(1, count), vm(nz, nx, ny), vm(3, nz, nx, ny),
-            vm(2, nz + 2, nx, ny), vm(2, nz, nx, ny), vm(nz, nx, ny), vm(nz, 4, nx, ny), vm(nz, 17, nx, ny), vm(3, nx, ny), vm(2, 3, nx, ny),
+            vm(2, nz + 2, nx, ny), vm(nz, nx, ny), vm(nz, nx, ny), vm(nz, 5, nx, ny), vm(nz, 17, nx, ny), vm(3, nx, ny), vm(2, 3, nx, ny),
             vm(5, nz + 2, nx, ny), vm(5, nz + 2, nx, ny), vm(2, nz + 2, nx, ny),
             vm(nz, nx, ny), vm(nz, nx, ny), vm(nz, nx, ny), vm(2, nz + 4, nx, ny), vm(2, nx, ny),
             *packs, vm(-(-2 // per), nx, ny), vm(-(-2 // per), nx, ny),

time: 26 us -> 25.8 us (level)
  no operation moved by 1% of the time
where the time goes in v8:
time: 25.8 us; the launch traced here: 25.7 us
  Pallas kernels  25 us (97%)
  between operations  0.64 us (2%)
    pallas_call x1, Pallas kernels, local(): pl.pallas_call(functools.partial(kernel, sizes), out_shape=jax.ShapeDtype...  24.4 us
    pallas_call x1, Pallas kernels, local(): pl.pallas_call(store, out_shape=(jax.ShapeDtypeStruct((nz, nx, ny), f32),...  0.64 us

profile of v8, /device:TPU:0, one launch (start us, length us, event | category | flops | bytes accessed | tf_op | source)
XLA Modules:
  0.0 25.7 jit_solution(11060273713328445946)
XLA Ops:
  0.6 24.4 %adjoint.1.result = f32[17,8,128]{2,1,0:T(8,128)S(1)} custom-call(f32[5,16,8,128]{3,2,1,0:T(8,128)} %st.1, f32[16,8,128]{2,1,0:T(8,128)} %ga.1, s32[2,16,8,128]{3,2,1,0:T(8,128)} %sw.1, s32[1,256]{1,0:T(1,128)} %bitcast.3, f32[1,256]{1,0:T(1,128)} %bitcast.4), custom_call_target="tpu_custom_call" | custom-call | tf_op jit(solution)/shard_map/adjoint/pallas_call | solution.py:621
  25.0 0.6 %store.1 = (f32[16,8,128]{2,1,0:T(8,128)}, f32[1,1]{1,0:T(1,128)}) custom-call(f32[17,8,128]{2,1,0:T(8,128)S(1)} %adjoint.1.result), custom_call_target="tpu_custom_call" | custom-call | tf_op jit(solution)/shard_map/store/pallas_call | solution.py:643

commit v9 on v8

--- a/solution.py
+++ b/solution.py
@@ -32,7 +32,7 @@
 
 def kernel(
     sizes, st, ga, sw, pr_in, ob_in, result,
-    se0, se1, ge, we, xs0, xg, xw, xs1, xt1, xq, q1, xv0, pr, ob, en0, ve0, xl, xm, xk, part, cof, ycof, zcof, az, bz, zm, kap, kah, sig,
+    se0, se1, ge, we, xs0, xg, xw, xs1, xt1, xq, q1, xv0, pr, ob, en0, ve0, xl, xm, mm, xk, part, cof, ycof, zcof, az, bz, zm, kap, kah, sig,
     lam, yr,
     yp1, yl1, yu1, yp2, yl2, yu2, yp3, yl3, yu3, el3, eu3, cnt, sob, vel, hot_a, hot_b, grad,
     mine, ar, local_sem, send_sem, recv_sem, all_send, all_recv,
@@ -223,7 +223,7 @@
     )
     extra = Exchange(rows_of(se1.at[pl.ds(2, 2)], xt1, 2))
     third = Exchange(
-        rows_of(lam, xl, 2, 0, 1) + rows_of(lam.at[1], xm, 2, 1) + rows_of(sig, xk, 0, 1)
+        rows_of(lam.at[1], xl.at[1], 2, 0, 1) + rows_of(mm, xm, 0) + rows_of(sig, xk, 0, 1)
         + planes_of(lam, 2, 2) + y_copies(yp3, yl3, yu3) + edge_copies()
     )
     exchanges = (first, later, second, extra, third)
@@ -391,7 +391,10 @@
         part[z, 2] = 0.5 * (above - below)
         part[z, 3] = we[1, z + 2].astype(jnp.float32) * QUAD * (1.0 + r)
         inv = 0.5 / (1.0 + r)
-        part[z, 4] = jnp.where(row < nx // 2, pltpu.roll(inv, 1, 0), pltpu.roll(inv, nx - 1, 0))
+        gamma = ge[z + 2]
+        pull = 0.5 * DT * ((2.0 - gamma) * v + gamma * (xs0[1, z] / (1.0 + xs0[0, z])))
+        for k, outer in ((4, inv), (5, pull)):
+            part[z, k] = jnp.where(row < nx // 2, pltpu.roll(outer, 1, 0), pltpu.roll(outer, nx - 1, 0))
         z_flux(z + 1)
         return carry
 
@@ -438,8 +441,11 @@
         lam0 = -w * v
         lam[0, z + 2] = lam0
         lam[1, z + 2] = w
-        sigma = DT * slope * (pltpu.roll(w, nx - 1, 0) - pltpu.roll(w, 1, 0))
-        sig[z] = 0.5 * DT * lam0 - part[z, 4] * sigma
+        next_row, last_row = pltpu.roll(w, nx - 1, 0), pltpu.roll(w, 1, 0)
+        sigma = DT * slope * (next_row - last_row)
+        weigh = jnp.where(row < nx // 2, 0.5 * DT * SIGNAL, -0.5 * DT * SIGNAL)
+        sig[z] = 0.5 * DT * lam0 - part[z, 4] * sigma + (weigh + part[z, 5]) * w
+        mm[z] = 0.5 * DT * lam0 + sign * DT * slope * (0.5 / rho_h) * jnp.where(row == 0, next_row, last_row)
         return carry
 
     loop(nz, step_two, 0, 16)
@@ -528,8 +534,8 @@
         return above, jnp.where(lane == 0, ghost, pltpu.roll(x, 1, 1))
 
     def adjoint(z, carry):
-        ca, cx, cy, cz, gy, gz, gg, gr, ci, ka, ky, kz, ki, dx, mx, my, rows = [cof[z, k] for k in range(17)]
-        l1, x0, x1, x2 = lam[1, z + 2], xl[0, z + 1], xl[1, z + 1], xm[z]
+        ca, cx, cy, cz, gy, gz, gg, gr, ci, _, ky, kz, ki, dx, mx, my, rows = [cof[z, k] for k in range(17)]
+        l1, x1 = lam[1, z + 2], xl[1, z + 1]
         zero = jnp.zeros_like(dx)
         y1 = jnp.where(at_side, side(yl3, 1, z), zero)
         y1_turn = sign_y * y1
@@ -537,17 +543,17 @@
         zu, zd, fu, fd = lam[1, z + 3], lam[1, z + 1], xl[1, z + 2], xl[1, z]
         dx = dx + sign * x1
         dz = zu - zd
-        sigma, sigma_h = kap[z] * dx, kah[z] * (sign * (x2 - l1))
+        sigma = kap[z] * dx
         en = gg * dx
         zm[0, z + 1] = half * (lam[0, z + 3] - lam[0, z + 1]) + cx * dz - gz * dx
         zm[1, z + 1] = en
         my = my + half * sign_y * side(yl3, 0, z) + cx * y1_turn - gy * dx
         mx = (
-            mx + weight * ((x1 + y1) + (zu + zd)) + half * sign * x0 + ca * dx + cy * y1_turn + cz * dz
-            + ci * (down(0, sigma, sigma_h) - up(0, sigma, sigma_h))
+            mx + weight * ((x1 + y1) + (zu + zd)) + ca * dx + cy * y1_turn + cz * dz
+            + ci * (down(0, sigma, zero) - up(0, sigma, zero)) + jnp.where(at_end, sign * xm[z] + ci * kah[z] * l1, zero)
         )
         rows = (
-            rows + (1.0 - 6.0 * weight) * x1 + weight * ((eu + ed) + (fu + fd)) + sign * xk[z] + ka * x2
+            rows + (1.0 - 6.0 * weight) * x1 + weight * ((eu + ed) + (fu + fd)) + sign * xk[z]
             + ky * (eu - ed) + kz * (fu - fd) + ki * sigma
         )
         rows = jnp.where(in_row, rows, zero)
@@ -628,7 +634,7 @@
             vm(5, nz, nx, ny), vm(nz, nx, ny), vm(2, nz, nx, ny, dtype=jnp.int32),
             vm(2, nz, nx, ny), vm(2, nz, nx, ny), vm(2, nz, nx, ny), vm(2, nz, nx, ny), vm(nz, nx, ny),
             vm(1, count, dtype=jnp.int32), vm(1, count), vm(nz, nx, ny), vm(3, nz, nx, ny),
-            vm(2, nz + 2, nx, ny), vm(nz, nx, ny), vm(nz, nx, ny), vm(nz, 5, nx, ny), vm(nz, 17, nx, ny), vm(3, nx, ny), vm(2, 3, nx, ny),
+            vm(2, nz + 2, nx, ny), vm(nz, nx, ny), vm(nz, nx, ny), vm(nz, nx, ny), vm(nz, 6, nx, ny), vm(nz, 17, nx, ny), vm(3, nx, ny), vm(2, 3, nx, ny),
             vm(5, nz + 2, nx, ny), vm(5, nz + 2, nx, ny), vm(2, nz + 2, nx, ny),
             vm(nz, nx, ny), vm(nz, nx, ny), vm(nz, nx, ny), vm(2, nz + 4, nx, ny), vm(2, nx, ny),
             *packs, vm(-(-2 // per), nx, ny), vm(-(-2 // per), nx, ny),

time: 25.8 us -> 25.7 us (level)
  no operation moved by 1% of the time
where the time goes in v9:
time: 25.7 us; the launch traced here: 25.5 us
  Pallas kernels  24.9 us (97%)
  between operations  0.64 us (2%)
    pallas_call x1, Pallas kernels, local(): pl.pallas_call(functools.partial(kernel, sizes), out_shape=jax.ShapeDtype...  24.2 us
    pallas_call x1, Pallas kernels, local(): pl.pallas_call(store, out_shape=(jax.ShapeDtypeStruct((nz, nx, ny), f32),...  0.64 us

profile of v9, /device:TPU:0, one launch (start us, length us, event | category | flops | bytes accessed | tf_op | source)
XLA Modules:
  0.0 25.5 jit_solution(12922330246545966134)
XLA Ops:
  0.6 24.2 %adjoint.1.result = f32[17,8,128]{2,1,0:T(8,128)S(1)} custom-call(f32[5,16,8,128]{3,2,1,0:T(8,128)} %st.1, f32[16,8,128]{2,1,0:T(8,128)} %ga.1, s32[2,16,8,128]{3,2,1,0:T(8,128)} %sw.1, s32[1,256]{1,0:T(1,128)} %bitcast.3, f32[1,256]{1,0:T(1,128)} %bitcast.4), custom_call_target="tpu_custom_call" | custom-call | tf_op jit(solution)/shard_map/adjoint/pallas_call | solution.py:627
  24.9 0.6 %store.1 = (f32[16,8,128]{2,1,0:T(8,128)}, f32[1,1]{1,0:T(1,128)}) custom-call(f32[17,8,128]{2,1,0:T(8,128)S(1)} %adjoint.1.result), custom_call_target="tpu_custom_call" | custom-call | tf_op jit(solution)/shard_map/store/pallas_call | solution.py:649

commit v10 on v9

--- a/solution.py
+++ b/solution.py
@@ -566,7 +566,7 @@
         grad[z] = gr * dx + en0[z] * pi
         return carry
 
-    loop(nz, adjoint, 0, 8)
+    loop(nz, adjoint, 0, 16)
 
     def along_z(z, acc):
         g = grad[z] + en0[z] * (zm[0, z + 2] - zm[0, z] + ve0[2, z] * (zm[1, z + 2] - zm[1, z]))

time: 25.7 us -> 25.8 us (level)
  no operation moved by 1% of the time
where the time goes in v10:
time: 25.8 us; the launch traced here: 25.7 us
  Pallas kernels  25.1 us (97%)
  between operations  0.64 us (2%)
    pallas_call x1, Pallas kernels, local(): pl.pallas_call(functools.partial(kernel, sizes), out_shape=jax.ShapeDtype...  24.4 us
    pallas_call x1, Pallas kernels, local(): pl.pallas_call(store, out_shape=(jax.ShapeDtypeStruct((nz, nx, ny), f32),...  0.64 us

profile of v10, /device:TPU:0, one launch (start us, length us, event | category | flops | bytes accessed | tf_op | source)
XLA Modules:
  0.0 25.7 jit_solution(11385109718187746426)
XLA Ops:
  0.6 24.4 %adjoint.1.result = f32[17,8,128]{2,1,0:T(8,128)S(1)} custom-call(f32[5,16,8,128]{3,2,1,0:T(8,128)} %st.1, f32[16,8,128]{2,1,0:T(8,128)} %ga.1, s32[2,16,8,128]{3,2,1,0:T(8,128)} %sw.1, s32[1,256]{1,0:T(1,128)} %bitcast.3, f32[1,256]{1,0:T(1,128)} %bitcast.4), custom_call_target="tpu_custom_call" | custom-call | tf_op jit(solution)/shard_map/adjoint/pallas_call | solution.py:627
  25.0 0.6 %store.1 = (f32[16,8,128]{2,1,0:T(8,128)}, f32[1,1]{1,0:T(1,128)}) custom-call(f32[17,8,128]{2,1,0:T(8,128)S(1)} %adjoint.1.result), custom_call_target="tpu_custom_call" | custom-call | tf_op jit(solution)/shard_map/store/pallas_call | solution.py:649
